TPU v7x, 32 devices: a whole 2x2x4 slice. The times are simulated.
32 devices in a mesh: dp: 8 (over z, x), mp: 4 (over y, core).
Axes of the slice: x: 2, y: 2, z: 4, core: 2. Of those that a mesh axis runs over, the one named last changes fastest.
Arguments:
- tokens: bfloat16 [2, 16384, 768], P(None, ('dp', 'mp')), may hold values from -6 to 6
- norm_gains: bfloat16 [768, 2], P('dp'), may hold values from 0.5 to 1.5
- norm_biases: bfloat16 [768, 2], P('dp'), may hold values from -3 to 3
- w_query: bfloat16 [768, 768], P('dp', 'mp'), may hold values from -0.21875 to 0.21875
- w_keyval: bfloat16 [768, 128], P('dp'), may hold values from -0.21875 to 0.21875
- w_output: bfloat16 [768, 768], P('dp', 'mp'), may hold values from -1.5 to 1.5
- w_up: bfloat16 [768, 3072], P('dp', 'mp'), may hold values from -0.21875 to 0.21875
- w_down: bfloat16 [768, 3072], P('dp', 'mp'), may hold values from -0.109375 to 0.109375
- cotangent: bfloat16 [2, 16384, 768], P(None, ('dp', 'mp')), may hold values from -6 to 6
- subset_ids: int32 [32768], P('dp'), may hold values from 0 to 21
- subset_weights: float32 [22], replicated, may hold values from 0.25 to 4
Outputs:
- output: bfloat16 [2, 16384, 768], P(None, ('dp', 'mp'))
- kv_cache: bfloat16 [32768, 128], P('dp')
- input_grad: bfloat16 [2, 16384, 768], P(None, ('dp', 'mp'))
- grad_gains: float32 [768, 2], P('dp')
- grad_biases: float32 [768, 2], P('dp')
- grad_query: float32 [768, 768], P('dp', 'mp')
- grad_keyval: float32 [768, 128], P('dp')
- grad_output: float32 [768, 768], P('dp', 'mp')
- grad_up: float32 [768, 3072], P('dp', 'mp')
- grad_down: float32 [768, 3072], P('dp', 'mp')
All inputs are finite; a program needn't handle non-finite values.
Results may differ from a plain program's by a relative error of at most 0.012.
Values may be sent and summed in bfloat16 or wider, within the bound.
A program may use at most 256 MiB of HBM per device.

v0:
```python
import jax
import jax.numpy as jnp
from jax import lax
from jax.sharding import PartitionSpec as P

HD = 64
ROT = 16
SEQ_LEN = 2048
QB = 512


epsilon = 1e-05
sqrt_half = 0.7071067811865476
inv_sqrt_two_pi = 0.3989422804014327


def rotary_tables():
    position = jnp.arange(SEQ_LEN, dtype=jnp.float32)
    frequency = 10000.0 ** (-2.0 * jnp.arange(ROT // 2, dtype=jnp.float32) / ROT)
    angles = position[:, None] * frequency[None, :]
    return (jnp.cos(angles), jnp.sin(angles))


def rotate(vectors, cosine, sine_table):
    first_half = vectors[..., : ROT // 2]
    second_half = vectors[..., ROT // 2 : ROT]
    cos_wide = cosine[:, None, :]
    sin_wide = sine_table[:, None, :]
    return jnp.concatenate(
        [
            first_half * cos_wide - second_half * sin_wide,
            second_half * cos_wide + first_half * sin_wide,
            vectors[..., ROT:],
        ],
        axis=-1,
    )


def causal_scores(query_block, key_rows, row_begin, finish):
    scores = jnp.einsum(
        "sqhd,skd->shqk", query_block, key_rows[:, :finish], preferred_element_type=jnp.float32
    )
    row_ids = row_begin + jnp.arange(QB, dtype=jnp.int32)
    col_ids = jnp.arange(finish, dtype=jnp.int32)
    causal = col_ids[None, :] <= row_ids[:, None]
    return jnp.where(causal, scores, -1e30)


def attention_forward(queries, key_rows, value_rows):
    blocks = SEQ_LEN // QB
    pieces = []
    log_norms = []
    for block_index in range(blocks):
        row_begin = block_index * QB
        finish = row_begin + QB
        scores = causal_scores(queries[:, row_begin:finish], key_rows, row_begin, finish)
        maximum = jnp.max(scores, axis=-1, keepdims=True)
        shifted = jnp.exp(scores - maximum)
        totals = jnp.sum(shifted, axis=-1, keepdims=True)
        probability = (shifted / totals).astype(jnp.bfloat16)
        pieces.append(
            jnp.einsum(
                "shqk,skd->sqhd",
                probability,
                value_rows[:, :finish],
                preferred_element_type=jnp.float32,
            )
        )
        log_norms.append(maximum + jnp.log(totals))
    return (jnp.concatenate(pieces, axis=1), log_norms)


def attention_backward(queries, key_rows, value_rows, log_norms, grad_heads):
    blocks = SEQ_LEN // QB
    length = key_rows.shape[1]
    query_pieces = []
    grad_keys = jnp.zeros(key_rows.shape, jnp.float32)
    grad_values = jnp.zeros(value_rows.shape, jnp.float32)
    for block_index in range(blocks):
        row_begin = block_index * QB
        finish = row_begin + QB
        query_block = queries[:, row_begin:finish]
        grad_block = grad_heads[:, row_begin:finish]
        scores = causal_scores(query_block, key_rows, row_begin, finish)
        probability = jnp.exp(scores - log_norms[block_index])
        grad_probs = jnp.einsum(
            "sqhd,skd->shqk", grad_block, value_rows[:, :finish], preferred_element_type=jnp.float32
        )
        inner_sum = jnp.sum(probability * grad_probs, axis=-1, keepdims=True)
        grad_scores = (probability * (grad_probs - inner_sum)).astype(jnp.bfloat16)
        query_pieces.append(
            jnp.einsum(
                "shqk,skd->sqhd",
                grad_scores,
                key_rows[:, :finish],
                preferred_element_type=jnp.float32,
            )
        )
        key_part = jnp.einsum(
            "shqk,sqhd->skd", grad_scores, query_block, preferred_element_type=jnp.float32
        )
        value_part = jnp.einsum(
            "shqk,sqhd->skd",
            probability.astype(jnp.bfloat16),
            grad_block,
            preferred_element_type=jnp.float32,
        )
        padding = ((0, 0), (0, length - finish), (0, 0))
        grad_keys = grad_keys + jnp.pad(key_part, padding)
        grad_values = grad_values + jnp.pad(value_part, padding)
    return (jnp.concatenate(query_pieces, axis=1), grad_keys, grad_values)


def shards(
    tokens,
    norm_gains,
    norm_biases,
    w_query,
    w_keyval,
    w_output,
    w_up,
    w_down,
    cotangent,
    subset_ids,
    subset_weights,
):
    micro_count = tokens.shape[0]
    own_rows = tokens.shape[1]
    micro_rows = subset_ids.shape[0] // micro_count
    sequences = micro_rows // SEQ_LEN
    head_count = w_query.shape[1] // HD
    kv_share = 1.0 / lax.axis_size("mp")
    own_begin = lax.axis_index("mp") * own_rows
    cosine, sine_table = rotary_tables()
    matches = subset_ids[:, None] == jnp.arange(subset_weights.shape[0], dtype=jnp.int32)[None, :]
    row_scale = jnp.sum(jnp.where(matches, subset_weights[None, :], 0.0), axis=1)
    outputs = []
    caches = []
    input_grads = []
    summed = None
    for micro_index in range(micro_count):
        row_begin = micro_index * micro_rows
        rows_in = tokens[micro_index]
        cot_rows = cotangent[micro_index]
        scale_rows = row_scale[row_begin : row_begin + micro_rows]
        own_scale = lax.dynamic_slice_in_dim(scale_rows, own_begin, own_rows, 0)
        gathered = (
            lax.all_gather(norm_gains, "dp", axis=0, tiled=True),
            lax.all_gather(norm_biases, "dp", axis=0, tiled=True),
            lax.all_gather(w_query, "dp", axis=0, tiled=True),
            lax.all_gather(w_keyval, "dp", axis=0, tiled=True),
            lax.all_gather(w_output, "dp", axis=0, tiled=True),
            lax.all_gather(w_up, "dp", axis=0, tiled=True),
            lax.all_gather(w_down, "dp", axis=0, tiled=True),
        )
        gains_full, biases_full, query_w, keyval_w, output_w, up_w, down_w = gathered
        rows_full = lax.all_gather(rows_in, "mp", axis=0, tiled=True).astype(jnp.float32)
        mean_row = jnp.mean(rows_full, axis=1, keepdims=True)
        centered = rows_full - mean_row
        inverse = lax.rsqrt(jnp.mean(centered * centered, axis=1, keepdims=True) + epsilon)
        normed = centered * inverse
        gains_float = gains_full.astype(jnp.float32)
        biases_float = biases_full.astype(jnp.float32)
        attn_in = (normed * gains_float[:, 0] + biases_float[:, 0]).astype(jnp.bfloat16)
        mlp_in = (normed * gains_float[:, 1] + biases_float[:, 1]).astype(jnp.bfloat16)
        query_pre = jnp.dot(attn_in, query_w, preferred_element_type=jnp.float32)
        keyval_pre = jnp.dot(attn_in, keyval_w, preferred_element_type=jnp.float32)
        queries = (
            rotate(query_pre.reshape(sequences, SEQ_LEN, head_count, HD), cosine, sine_table)
            * HD ** (-0.5)
        ).astype(jnp.bfloat16)
        key_rows = (
            rotate(keyval_pre[:, :HD].reshape(sequences, SEQ_LEN, 1, HD), cosine, sine_table)
            .astype(jnp.bfloat16)
            .reshape(sequences, SEQ_LEN, HD)
        )
        value_rows = keyval_pre[:, HD:].astype(jnp.bfloat16).reshape(sequences, SEQ_LEN, HD)
        caches.append(jnp.concatenate([key_rows, value_rows], axis=-1).reshape(micro_rows, 2 * HD))
        mixed_heads, log_norms = attention_forward(queries, key_rows, value_rows)
        heads_out = mixed_heads.reshape(micro_rows, head_count * HD).astype(jnp.bfloat16)
        hidden_pre = jnp.dot(mlp_in, up_w, preferred_element_type=jnp.float32)
        hidden = jax.nn.gelu(hidden_pre, approximate=False).astype(jnp.bfloat16)
        branch_sum = jnp.einsum(
            "rc,dc->rd", heads_out, output_w, preferred_element_type=jnp.float32
        ) + jnp.einsum("rf,df->rd", hidden, down_w, preferred_element_type=jnp.float32)
        reduced_out = lax.psum_scatter(branch_sum, "mp", scatter_dimension=0, tiled=True)
        outputs.append((reduced_out + rows_in.astype(jnp.float32)).astype(jnp.bfloat16))
        gathered_back = (
            lax.all_gather(norm_gains, "dp", axis=0, tiled=True),
            lax.all_gather(w_query, "dp", axis=0, tiled=True),
            lax.all_gather(w_keyval, "dp", axis=0, tiled=True),
            lax.all_gather(w_output, "dp", axis=0, tiled=True),
            lax.all_gather(w_up, "dp", axis=0, tiled=True),
            lax.all_gather(w_down, "dp", axis=0, tiled=True),
        )
        gains_back, query_back, keyval_back, output_back, up_back, down_back = gathered_back
        cot_full = lax.all_gather(cot_rows, "mp", axis=0, tiled=True).astype(jnp.float32)
        grad_low = (cot_full * scale_rows[:, None]).astype(jnp.bfloat16)
        grad_hidden = jnp.dot(grad_low, down_back, preferred_element_type=jnp.float32)
        normal_cdf = 0.5 * (1.0 + jax.scipy.special.erf(hidden_pre * sqrt_half))
        density = jnp.exp(-0.5 * hidden_pre * hidden_pre) * inv_sqrt_two_pi
        grad_hidden_pre = (grad_hidden * (normal_cdf + hidden_pre * density)).astype(jnp.bfloat16)
        grad_down = jnp.einsum("rd,rf->df", grad_low, hidden, preferred_element_type=jnp.float32)
        grad_up = jnp.einsum(
            "rd,rf->df", mlp_in, grad_hidden_pre, preferred_element_type=jnp.float32
        )
        grad_mlp_in = jnp.einsum(
            "rf,df->rd", grad_hidden_pre, up_back, preferred_element_type=jnp.float32
        )
        grad_heads = jnp.dot(grad_low, output_back, preferred_element_type=jnp.float32).astype(
            jnp.bfloat16
        )
        grad_output = jnp.einsum(
            "rd,rc->dc", grad_low, heads_out, preferred_element_type=jnp.float32
        )
        grad_queries, grad_keys, grad_values = attention_backward(
            queries,
            key_rows,
            value_rows,
            log_norms,
            grad_heads.reshape(sequences, SEQ_LEN, head_count, HD),
        )
        grad_query_pre = (
            (rotate(grad_queries, cosine, -sine_table) * HD ** (-0.5))
            .astype(jnp.bfloat16)
            .reshape(micro_rows, head_count * HD)
        )
        grad_query = jnp.einsum(
            "rd,rc->dc", attn_in, grad_query_pre, preferred_element_type=jnp.float32
        )
        grad_attn_query = jnp.einsum(
            "rc,dc->rd", grad_query_pre, query_back, preferred_element_type=jnp.float32
        )
        gain_part = jnp.stack(
            [jnp.sum(grad_attn_query * normed, axis=0), jnp.sum(grad_mlp_in * normed, axis=0)],
            axis=1,
        )
        bias_part = jnp.stack(
            [jnp.sum(grad_attn_query, axis=0), jnp.sum(grad_mlp_in, axis=0)], axis=1
        )
        keyval_part = jnp.concatenate([grad_keys, grad_values], axis=-1).reshape(micro_rows, 2 * HD)
        keyval_sum, gain_sum, bias_sum = lax.psum((keyval_part, gain_part, bias_part), "mp")
        grad_key_pre = rotate(
            keyval_sum[:, :HD].reshape(sequences, SEQ_LEN, 1, HD), cosine, -sine_table
        ).reshape(micro_rows, HD)
        grad_keyval_pre = jnp.concatenate([grad_key_pre, keyval_sum[:, HD:]], axis=1).astype(
            jnp.bfloat16
        )
        grad_keyval = jnp.einsum(
            "rd,rc->dc", attn_in, grad_keyval_pre, preferred_element_type=jnp.float32
        )
        grad_attn_keyval = jnp.einsum(
            "rc,dc->rd", grad_keyval_pre, keyval_back, preferred_element_type=jnp.float32
        )
        kv_gain = jnp.sum(grad_attn_keyval * normed, axis=0)
        kv_bias = jnp.sum(grad_attn_keyval, axis=0)
        grad_gains = gain_sum + jnp.stack([kv_gain, jnp.zeros_like(kv_gain)], axis=1)
        grad_biases = bias_sum + jnp.stack([kv_bias, jnp.zeros_like(kv_bias)], axis=1)
        grad_attn_in = grad_attn_query + kv_share * grad_attn_keyval
        gains_back_float = gains_back.astype(jnp.float32)
        grad_normed = grad_attn_in * gains_back_float[:, 0] + grad_mlp_in * gains_back_float[:, 1]
        centered_grad = (
            grad_normed
            - jnp.mean(grad_normed, axis=1, keepdims=True)
            - normed * jnp.mean(grad_normed * normed, axis=1, keepdims=True)
        )
        reduced_grad = lax.psum_scatter(
            centered_grad * inverse, "mp", scatter_dimension=0, tiled=True
        )
        local_rows = cot_rows.astype(jnp.float32) * own_scale[:, None]
        input_grads.append((reduced_grad + local_rows).astype(jnp.bfloat16))
        local_grads = (
            grad_gains,
            grad_biases,
            grad_query,
            grad_keyval,
            grad_output,
            grad_up,
            grad_down,
        )
        reduced = (
            lax.psum_scatter(local_grads[0], "dp", scatter_dimension=0, tiled=True),
            lax.psum_scatter(local_grads[1], "dp", scatter_dimension=0, tiled=True),
            lax.psum_scatter(local_grads[2], "dp", scatter_dimension=0, tiled=True),
            lax.psum_scatter(local_grads[3], "dp", scatter_dimension=0, tiled=True),
            lax.psum_scatter(local_grads[4], "dp", scatter_dimension=0, tiled=True),
            lax.psum_scatter(local_grads[5], "dp", scatter_dimension=0, tiled=True),
            lax.psum_scatter(local_grads[6], "dp", scatter_dimension=0, tiled=True),
        )
        summed = (
            reduced
            if summed is None
            else tuple((running + added for running, added in zip(summed, reduced)))
        )
    return (
        jnp.stack(outputs, axis=0),
        jnp.concatenate(caches, axis=0),
        jnp.stack(input_grads, axis=0),
        summed[0],
        summed[1],
        summed[2],
        summed[3],
        summed[4],
        summed[5],
        summed[6],
    )


def solution(mesh):
    return jax.shard_map(
        shards,
        mesh=mesh,
        in_specs=(
            P(None, ("dp", "mp"), None),
            P("dp", None),
            P("dp", None),
            P("dp", "mp"),
            P("dp", None),
            P("dp", "mp"),
            P("dp", "mp"),
            P("dp", "mp"),
            P(None, ("dp", "mp"), None),
            P("dp"),
            P(),
        ),
        out_specs=(
            P(None, ("dp", "mp"), None),
            P("dp", None),
            P(None, ("dp", "mp"), None),
            P("dp", None),
            P("dp", None),
            P("dp", "mp"),
            P("dp", None),
            P("dp", "mp"),
            P("dp", "mp"),
            P("dp", "mp"),
        ),
        check_vma=False,
    )
```

profile of v0, /device:TPU:0, one launch (start us, length us, event | category | flops | bytes accessed | tf_op | source)
XLA Modules:
  0.0 1251.4 jit_solution(10996470224705625093)
XLA Ops:
  15.4 22.3 %all-gather.4 = bf16[8,96,2]{1,2,0:T(2,128)(2,1)S(1)} all-gather(bf16[1,96,2]{1,2,0:T(2,128)(2,1)S(1)} %bitcast.1078), channel_id=1, replica_groups=mesh['dp'=8,'mp'=4] {'dp'}, dimensions={0}, use_global_device_ids=true | all-gather | bytes 3456 | tf_op jit(solution)/shard_map/all_gather | solution.py:148
  38.4 16.3 %all-gather.5 = bf16[8,96,2]{1,2,0:T(2,128)(2,1)S(1)} all-gather(bf16[1,96,2]{1,2,0:T(2,128)(2,1)S(1)} %bitcast.1079), channel_id=1, replica_groups=mesh['dp'=8,'mp'=4] {'dp'}, dimensions={0}, use_global_device_ids=true | all-gather | bytes 3456 | tf_op jit(solution)/shard_map/all_gather | solution.py:149
  55.5 32.6 %all_gather.25 = bf16[768,128]{1,0:T(8,128)(2,1)} all-gather(bf16[96,128]{1,0:T(8,128)(2,1)S(1)} %copy-done.158), channel_id=1, replica_groups=mesh['dp'=8,'mp'=4] {'dp'}, dimensions={0}, use_global_device_ids=true | all-gather | bytes 221184 | tf_op jit(solution)/shard_map/all_gather | solution.py:151
  89.1 33.2 %all_gather.26 = bf16[768,192]{1,0:T(8,128)(2,1)} all-gather(bf16[96,192]{1,0:T(8,128)(2,1)S(1)} %copy-done.148), channel_id=1, replica_groups=mesh['dp'=8,'mp'=4] {'dp'}, dimensions={0}, use_global_device_ids=true | all-gather | bytes 331776 | tf_op jit(solution)/shard_map/all_gather | solution.py:150
  122.3 33.3 %all_gather.27 = bf16[768,192]{1,0:T(8,128)(2,1)} all-gather(bf16[96,192]{1,0:T(8,128)(2,1)S(1)} %copy-done.149), channel_id=1, replica_groups=mesh['dp'=8,'mp'=4] {'dp'}, dimensions={0}, use_global_device_ids=true | all-gather | bytes 331776 | tf_op jit(solution)/shard_map/all_gather | solution.py:152
  235.2 6.4 fusion.142
  269.9 6.7 fusion.13
  281.6 11.7 fusion.126
  293.3 11.3 fusion.127
  317.4 6.3 fusion.281
  335.5 15.2 %fusion.3 = (f32[3,512]{1,0:T(4,128)}, f32[3,512]{1,0:T(4,128)}, f32[2048,512,3]{1,0,2:T(8,128)}) fusion(f32[2048,512,3]{1,0,2:T(8,128)} %copy-done.2, f32[3,512]{1,0:T(4,128)S(1)} %log_add_fusion.4, pred[512,2048]{0,1:T(8,128)(4,1)S(1)} %copy-done.7, f32[2048,512,3]{1,0,2:T(8,128)S(1)} %fusion.296, bf16[1,2048,3,64]{1,3,2,0:T(8,128)(2,1)} %bitcast.1072, ...), kind=kOutput, calls=%fused_computation.9 | convolution fusion | flops 421524480 | bytes 39274496 | tf_op jit(solution)/shard_map/sqhd,skd->shqk/dot_general | solution.py:86
  355.6 18.4 %fusion.84 = (bf16[3,512,2048]{1,2,0:T(8,128)(2,1)S(1)}, f32[3,512]{1,0:T(4,128)S(1)}) fusion(f32[2048,512,3]{1,0,2:T(8,128)} %get-tuple-element.174, f32[2048,512,3]{1,0,2:T(8,128)} %copy-done.2, f32[3,512]{1,0:T(4,128)} %get-tuple-element.76, f32[3,512]{1,0:T(4,128)} %copy-done.133, pred[512,2048]{0,1:T(8,128)(4,1)} %iota_compare_fusion, ...), kind=kLoop, calls=%fused_computation.116 | loop fusion | flops 28310016 | bytes 57696256 | tf_op jit(solution)/shard_map/reshape.130
  374.1 12.5 fusion.85
  418.9 7.1 fusion.253
  426.2 19.3 %fusion.68 = (bf16[2048,768]{1,0:T(8,128)(2,1)}, f32[2048,768]{1,0:T(8,128)}) fusion(bf16[768,768]{1,0:T(8,128)(2,1)} %all-gather.13.cloned.1.call-done, bf16[1,2048,768]{2,1,0:T(8,128)(2,1)} %all-gather.17.cloned.1.call-done, f32[768]{0:T(1024)S(1)} %copy-done.172, f32[768]{0:T(1024)S(1)} %copy-done.168, f32[2048]{0:T(1024)S(1)} %copy-done.144, ...), kind=kOutput, calls=%fused_computation.100 | convolution fusion | flops 2527592448 | bytes 13785088 | tf_op jit(solution)/shard_map/dot_general | solution.py:181
  445.6 17.8 %fusion.71 = (bf16[2048,768]{1,0:T(8,128)(2,1)}, f32[2048,768]{1,0:T(8,128)}) fusion(bf16[768,768]{1,0:T(8,128)(2,1)S(1)} %copy-done.180, bf16[1,2048,768]{2,1,0:T(8,128)(2,1)S(1)} %copy-done.16, f32[2048]{0:T(1024)S(1)} %copy-done.140, f32[2048]{0:T(1024)S(1)} %copy-done.127, f32[768]{0:T(1024)S(1)} %copy-done.172, f32[768]{0:T(1024)S(1)} %copy-done.168), kind=kOutput, calls=%fused_computation.103 | convolution fusion | flops 2527592448 | bytes 13785088 | tf_op jit(solution)/shard_map/dot_general | solution.py:181
  463.4 7.6 fusion.77
  500.0 11.5 fusion.357
  511.7 7.3 fusion.354
  519.2 10.3 all-reduce.16
  531.5 6.5 convolution_add_fusion.1
  568.4 6.3 fusion.38
  624.8 31.7 %reduce-scatter.36.cloned.1.call-done = f32[96,2]{1,0:T(8,128)} async-done(((f32[768,2]{1,0:T(8,128)}), f32[96,2]{1,0:T(8,128)}) %reduce-scatter.36.cloned.1.call-update) | async-done | bytes 784
  658.0 58.9 %reduce-scatter.16.cloned.1.call-done = f32[512,768]{1,0:T(8,128)} async-done(((f32[2048,768]{1,0:T(8,128)}), f32[512,768]{1,0:T(8,128)}) %reduce-scatter.16.cloned.1.call-update) | async-done | bytes 1572880 | tf_op jit(solution)/shard_map/reduce_scatter | solution.py:186
  716.8 61.4 %reduce-scatter.18.cloned.1.call-done = f32[512,768]{1,0:T(8,128)} async-done(((f32[2048,768]{1,0:T(8,128)}), f32[512,768]{1,0:T(8,128)}) %reduce-scatter.18.cloned.1.call-update) | async-done | bytes 1572880 | tf_op jit(solution)/shard_map/reduce_scatter | solution.py:186
  781.8 57.8 %reduce-scatter.22.cloned.1.call-done = f32[512,768]{1,0:T(8,128)} async-done(((f32[2048,768]{1,0:T(8,128)}), f32[512,768]{1,0:T(8,128)}) %reduce-scatter.22.cloned.1.call-update) | async-done | bytes 1572880 | tf_op jit(solution)/shard_map/reduce_scatter | solution.py:267
  839.6 61.4 %reduce-scatter.20.cloned.1.call-done = f32[512,768]{1,0:T(8,128)} async-done(((f32[2048,768]{1,0:T(8,128)}), f32[512,768]{1,0:T(8,128)}) %reduce-scatter.20.cloned.1.call-update) | async-done | bytes 1572880 | tf_op jit(solution)/shard_map/reduce_scatter | solution.py:267
  904.6 63.4 %reduce-scatter.28.cloned.1.call-done = f32[96,192]{1,0:T(8,128)} async-done(((f32[768,192]{1,0:T(8,128)}), f32[96,192]{1,0:T(8,128)}) %reduce-scatter.28.cloned.1.call-update) | async-done | bytes 73744 | tf_op jit(solution)/shard_map/reduce_scatter | solution.py:286
  968.0 66.1 %reduce-scatter.24.cloned.1.call-done = f32[96,192]{1,0:T(8,128)} async-done(((f32[768,192]{1,0:T(8,128)}), f32[96,192]{1,0:T(8,128)}) %reduce-scatter.24.cloned.1.call-update) | async-done | bytes 73744 | tf_op jit(solution)/shard_map/reduce_scatter | solution.py:284
  1034.1 65.0 %reduce-scatter.26.cloned.1.call-done = f32[96,128]{1,0:T(8,128)} async-done(((f32[768,128]{1,0:T(8,128)}), f32[96,128]{1,0:T(8,128)}) %reduce-scatter.26.cloned.1.call-update) | async-done | bytes 49168 | tf_op jit(solution)/shard_map/reduce_scatter | solution.py:285
  1099.1 72.5 %reduce-scatter.32.cloned.1.call-done = f32[96,768]{1,0:T(8,128)} async-done(((f32[768,768]{1,0:T(8,128)}), f32[96,768]{1,0:T(8,128)}) %reduce-scatter.32.cloned.1.call-update) | async-done | bytes 294928 | tf_op jit(solution)/shard_map/reduce_scatter | solution.py:288
  1171.6 72.7 %reduce-scatter.30.cloned.1.call-done = f32[96,768]{1,0:T(8,128)} async-done(((f32[768,768]{1,0:T(8,128)}), f32[96,768]{1,0:T(8,128)}) %reduce-scatter.30.cloned.1.call-update) | async-done | bytes 294928 | tf_op jit(solution)/shard_map/reduce_scatter | solution.py:287
  (661 shorter events, 303.1 us)
Async XLA Ops:
  7.2 31.2 %copy-start.177 = (bf16[96,2]{0,1:T(2,128)(2,1)S(1)}, bf16[96,2]{0,1:T(2,128)(2,1)}, u32[]{:S(2)}) copy-start(bf16[96,2]{0,1:T(2,128)(2,1)} %param.13) | copy-start | bytes 1156
  7.2 48.1 %copy-start.175 = (f32[22]{0:T(128)S(1)}, f32[22]{0:T(128)}, u32[]{:S(2)}) copy-start(f32[22]{0:T(128)} %param.21) | copy-start | bytes 268
  7.2 48.1 %copy-start.161 = (s32[4096]{0:T(1024)S(1)}, s32[4096]{0:T(1024)}, u32[]{:S(2)}) copy-start(s32[4096]{0:T(1024)} %param.20) | copy-start | bytes 49156
  7.2 48.3 %copy-start.158 = (bf16[96,128]{1,0:T(8,128)(2,1)S(1)}, bf16[96,128]{1,0:T(8,128)(2,1)}, u32[]{:S(2)}) copy-start(bf16[96,128]{1,0:T(8,128)(2,1)} %param.15) | copy-start | bytes 73732
  7.2 81.9 %copy-start.148 = (bf16[96,192]{1,0:T(8,128)(2,1)S(1)}, bf16[96,192]{1,0:T(8,128)(2,1)}, u32[]{:S(2)}) copy-start(bf16[96,192]{1,0:T(8,128)(2,1)} %param.14) | copy-start | bytes 110596
  7.2 115.1 %copy-start.149 = (bf16[96,192]{1,0:T(8,128)(2,1)S(1)}, bf16[96,192]{1,0:T(8,128)(2,1)}, u32[]{:S(2)}) copy-start(bf16[96,192]{1,0:T(8,128)(2,1)} %param.16) | copy-start | bytes 110596
  7.2 152.8 %all-gather.19.cloned.1.call-start = ((), (), s32[]{:S(2)}) async-start(), calls=%async_computation.18 | async-start | bytes 3932160 | tf_op jit(solution)/shard_map/all_gather | solution.py:157
  9.9 155.6 %all-gather.17.cloned.1.call-start = ((), (), s32[]{:S(2)}) async-start(), calls=%async_computation.17 | async-start | bytes 3932160 | tf_op jit(solution)/shard_map/all_gather | solution.py:157
  10.7 178.5 %all-gather.21.cloned.1.call-start = ((), (), s32[]{:S(2)}) async-start(), calls=%async_computation.19 | async-start | bytes 3932160 | tf_op jit(solution)/shard_map/all_gather | solution.py:197
  13.4 188.3 %all-gather.23.cloned.1.call-start = ((), (), s32[]{:S(2)}) async-start(), calls=%async_computation.20 | async-start | bytes 3932160 | tf_op jit(solution)/shard_map/all_gather | solution.py:197
  14.0 412.1 %all-gather.13.cloned.1.call-start = ((), (), s32[]{:S(2)}) async-start(), calls=%async_computation.11 | async-start | bytes 1327104 | tf_op jit(solution)/shard_map/all_gather | solution.py:153
  14.6 448.8 %all-gather.15.cloned.1.call-start = ((), (), s32[]{:S(2)}) async-start(), calls=%async_computation.12 | async-start | bytes 1327104 | tf_op jit(solution)/shard_map/all_gather | solution.py:154
  15.2 479.8 %all-reduce.20.cloned.1.call-start = ((), (), s32[]{:S(2)}) async-start(), calls=%async_computation.28 | async-start | bytes 4194304 | tf_op jit(solution)/shard_map/psum | solution.py:242
  15.2 144.8 %copy-start.165 = (f32[8]{0:T(128)}, f32[8]{0:T(128)S(1)}, u32[]{:S(2)}) copy-start(f32[8]{0:T(128)S(1)} %multiply_power_fusion) | copy-start | bytes 100
  15.4 195.1 %copy-start.28 = (pred[512,512]{0,1:T(8,128)(4,1)}, pred[512,512]{0,1:T(8,128)(4,1)S(1)}, u32[]{:S(2)}) copy-start(pred[512,512]{0,1:T(8,128)(4,1)S(1)} %iota_compare_fusion.4) | copy-start | bytes 786436
  38.4 132.8 %copy-start.159 = (f32[768]{0:T(1024)}, f32[768]{0:T(1024)S(1)}, u32[]{:S(2)}) copy-start(f32[768]{0:T(1024)S(1)} %get-tuple-element.84) | copy-start | bytes 9220
  55.5 133.8 %copy-start.162 = (f32[2048]{0:T(1024)}, f32[2048]{0:T(1024)S(1)}, u32[]{:S(2)}) copy-start(f32[2048]{0:T(1024)S(1)} %get-tuple-element.152) | copy-start | bytes 24580
  55.5 146.3 %copy-start.114 = (f32[2048]{0:T(1024)}, f32[2048]{0:T(1024)S(1)}, u32[]{:S(2)}) copy-start(f32[2048]{0:T(1024)S(1)} %get-tuple-element.151) | copy-start | bytes 24580
  89.1 94.3 %copy-start.90 = (f32[2048,8]{0,1:T(8,128)}, f32[2048,8]{0,1:T(8,128)S(1)}, u32[]{:S(2)}) copy-start(f32[2048,8]{0,1:T(8,128)S(1)} %get-tuple-element.159) | copy-start | bytes 196612
  426.0 197.3 %reduce-scatter.34.cloned.1.call-start = ((), (), s32[]{:S(2)}) async-start(), calls=%async_computation.26 | async-start | bytes 442368
  530.4 126.1 %reduce-scatter.36.cloned.1.call-start = ((), (), s32[]{:S(2)}) async-start(), calls=%async_computation.27 | async-start | bytes 442368
  531.4 185.4 %reduce-scatter.16.cloned.1.call-start = ((), (), s32[]{:S(2)}) async-start(), calls=%async_computation.13 | async-start | bytes 7864320 | tf_op jit(solution)/shard_map/reduce_scatter | solution.py:186
  538.0 240.3 %reduce-scatter.18.cloned.1.call-start = ((), (), s32[]{:S(2)}) async-start(), calls=%async_computation.14 | async-start | bytes 7864320 | tf_op jit(solution)/shard_map/reduce_scatter | solution.py:186
  561.0 278.6 %reduce-scatter.22.cloned.1.call-start = ((), (), s32[]{:S(2)}) async-start(), calls=%async_computation.16 | async-start | bytes 7864320 | tf_op jit(solution)/shard_map/reduce_scatter | solution.py:267
  568.3 332.7 %reduce-scatter.20.cloned.1.call-start = ((), (), s32[]{:S(2)}) async-start(), calls=%async_computation.15 | async-start | bytes 7864320 | tf_op jit(solution)/shard_map/reduce_scatter | solution.py:267
  574.7 393.3 %reduce-scatter.28.cloned.1.call-start = ((), (), s32[]{:S(2)}) async-start(), calls=%async_computation.23 | async-start | bytes 884736 | tf_op jit(solution)/shard_map/reduce_scatter | solution.py:286
  581.5 452.6 %reduce-scatter.24.cloned.1.call-start = ((), (), s32[]{:S(2)}) async-start(), calls=%async_computation.21 | async-start | bytes 884736 | tf_op jit(solution)/shard_map/reduce_scatter | solution.py:284
  588.9 510.1 %reduce-scatter.26.cloned.1.call-start = ((), (), s32[]{:S(2)}) async-start(), calls=%async_computation.22 | async-start | bytes 442368 | tf_op jit(solution)/shard_map/reduce_scatter | solution.py:285
  595.7 575.9 %reduce-scatter.32.cloned.1.call-start = ((), (), s32[]{:S(2)}) async-start(), calls=%async_computation.25 | async-start | bytes 2654208 | tf_op jit(solution)/shard_map/reduce_scatter | solution.py:288
  605.9 638.4 %reduce-scatter.30.cloned.1.call-start = ((), (), s32[]{:S(2)}) async-start(), calls=%async_computation.24 | async-start | bytes 2654208 | tf_op jit(solution)/shard_map/reduce_scatter | solution.py:287
  616.9 161.4 %copy-start.40 = (bf16[2,512,768]{2,1,0:T(8,128)(2,1)S(1)}, bf16[2,512,768]{2,1,0:T(8,128)(2,1)}, u32[]{:S(2)}) copy-start(bf16[2,512,768]{2,1,0:T(8,128)(2,1)} %param.11) | copy-start | bytes 4718596
  621.0 280.0 %copy-start.41 = (bf16[2,512,768]{2,1,0:T(8,128)(2,1)S(1)}, bf16[2,512,768]{2,1,0:T(8,128)(2,1)}, u32[]{:S(2)}) copy-start(bf16[2,512,768]{2,1,0:T(8,128)(2,1)} %param.19) | copy-start | bytes 4718596
  (198 other events, 1285.4 us)
Sparse Core Ops, SparseCore 0:
  10.2 31.2 all-gather.18
  43.6 28.4 all-gather.16
  73.7 28.4 all-gather.20
  103.7 28.4 all-gather.22
  134.2 40.9 all-gather.12
  177.3 39.8 all-gather.14
  426.2 50.6 all-reduce.19
  530.5 61.4 reduce-scatter.33
  595.3 61.2 reduce-scatter.35
  658.9 57.8 reduce-scatter.15
  719.4 58.8 reduce-scatter.17
  780.7 58.8 reduce-scatter.21
  842.1 58.8 reduce-scatter.19
  904.8 63.1 reduce-scatter.27
  971.7 62.2 reduce-scatter.23
  1037.7 61.2 reduce-scatter.25
  1103.0 68.5 reduce-scatter.31
  1175.5 68.7 reduce-scatter.29
where the time goes:
time: 1260 us; the launch traced here: 1250 us
  waiting for transfers between devices  614 us (49%)
  matrix products  304 us (24%)
  blocking collectives  148 us (12%)
  other arithmetic  135 us (11%)
  local copies, waits for them, and re-layouts  32.3 us (3%)
  between operations  17.6 us (1%)
    reduce_scatter x2, waiting for transfers between devices, shards(): lax.psum_scatter(branch_sum, 'mp', scatter_dimension=0, tiled=True)  120 us
    reduce_scatter x2, waiting for transfers between devices, shards(): lax.psum_scatter(centered_grad * inverse, 'mp', scatter_dimension=0, tile...  119 us
    reduce_scatter x1, waiting for transfers between devices, shards(): lax.psum_scatter(local_grads[5], 'dp', scatter_dimension=0, tiled=True)  72.7 us
    reduce_scatter x1, waiting for transfers between devices, shards(): lax.psum_scatter(local_grads[6], 'dp', scatter_dimension=0, tiled=True)  72.5 us
    another operation x12, other arithmetic  66.7 us
    reduce_scatter x1, waiting for transfers between devices, shards(): lax.psum_scatter(local_grads[2], 'dp', scatter_dimension=0, tiled=True)  66.1 us
    reduce_scatter x1, waiting for transfers between devices, shards(): lax.psum_scatter(local_grads[3], 'dp', scatter_dimension=0, tiled=True)  65 us
    reduce_scatter x1, waiting for transfers between devices, shards(): lax.psum_scatter(local_grads[4], 'dp', scatter_dimension=0, tiled=True)  63.4 us
  transfers between devices with their start and end apart: 18, of which 10 were waited for; matrix products, arithmetic and copies ran while one was open for 35% of the time, Pallas kernels for 0%

commit v1 on v0

v1 whole, which is shorter than its diff:
```python
import functools

import jax
import jax.numpy as jnp
from jax import lax
from jax.experimental import pallas as pl
from jax.experimental.pallas import tpu as pltpu
from jax.sharding import PartitionSpec as P

f32 = jnp.float32
bf = jnp.bfloat16
MESH = pl.DeviceIdType.MESH
HD = 64
ROT = 16
SEQ_LEN = 2048
epsilon = 1e-05
sqrt_half = 0.7071067811865476
inv_sqrt_two_pi = 0.3989422804014327


def coords(nz):
    d=lax.axis_index("dp"); m=lax.axis_index("mp")
    return d//2, d%2, m//2, m%2

def peer(pos,kind,nz):
    z,x,y,c=pos
    if kind[0]=="z": z=lax.rem(z+int(kind[1:]),nz)
    if kind=="x": x=1-x
    if kind=="y": y=1-y
    if kind=="c": c=1-c
    return (z*2+x, y*2+c)

def greet(pos,kinds,nz):
    bar=pltpu.get_barrier_semaphore()
    for k in kinds:
        pl.semaphore_signal(bar,inc=1,device_id=peer(pos,k,nz),device_id_type=MESH)
    pl.semaphore_wait(bar,len(kinds))

def gather_routes(order,nz):
    zs=[f"z{k}" for k in range(1,nz)]
    out=[]
    if order=="zyx":
        out.append(((0,0,0),zs+["y","x","c"]))
        out+=[((k,0,0),["y","x","c"]) for k in range(1,nz)]
        out+=[((k,0,1),["x","c"]) for k in range(nz)]
        out+=[((k,1,r),["c"]) for r in (0,1) for k in range(nz)]
    elif order=="xzy":
        out.append(((0,0,0),["x"]+zs+["y","c"]))
        out.append(((0,1,0),zs+["y","c"]))
        out+=[((k,r,0),["y","c"]) for k in range(1,nz) for r in (0,1)]
        out+=[((k,r,1),["c"]) for k in range(nz) for r in (0,1)]
    elif order=="zx":
        out.append(((0,0,0),zs+["x"]))
        out+=[((k,0,0),["x"]) for k in range(1,nz)]
        out+=[((k,1,0),[]) for k in range(nz)]
    return out

def gather_kernel(nz,plan,n,*refs):
    shards=refs[:n]; full=refs[n:2*n]; send,recv,local=refs[2*n:]
    pos=coords(nz); z,x,y,c=pos
    kinds=[f"z{k}" for k in range(1,nz)]+["x","y","c"]
    greet(pos,kinds,nz)
    sent=[]
    def block(i,lo,hi,zz,xx,yy,cc,both):
        d=zz*2+xx
        return full[i].at[yy*2+cc,d,:,lo:hi] if both else full[i].at[d,:,lo:hi]
    locs=[]
    for i in range(n):
        both=len(full[i].shape)==4
        dst=full[i].at[y*2+c,z*2+x] if both else full[i].at[z*2+x]
        cp=pltpu.make_async_copy(shards[i],dst,local.at[i]); cp.start(); locs.append(cp)
    chunks=[]
    count=0
    for ci,(i,lo,hi,order) in enumerate(plan):
        both=len(full[i].shape)==4
        chunks.append((ci,i,lo,hi,both,gather_routes(order,nz)))
    def act(chunk,step):
        nonlocal count
        ci,i,lo,hi,both,routes=chunk
        (k,rx,ry),fw=routes[step]
        zz=lax.rem(z+nz-k,nz); xx=1-x if rx else x; yy=1-y if ry else y
        dst=block(i,lo,hi,zz,xx,yy,c,both)
        midx=yy*2+c if both else 0
        if step>0:
            pltpu.make_async_remote_copy(dst,dst,send.at[0],recv.at[ci,midx,zz*2+xx],device_id=peer(pos,"c",nz),device_id_type=MESH).wait_recv()
        src=shards[i].at[:,lo:hi] if step==0 else dst
        for f in fw:
            cp=pltpu.make_async_remote_copy(src,dst,send.at[count],recv.at[ci,midx,zz*2+xx],device_id=peer(pos,f,nz),device_id_type=MESH)
            cp.start(); sent.append(cp); count+=1
    for ch in chunks: act(ch,0)
    longest=max(len(ch[5]) for ch in chunks)
    done=[1]*len(chunks)
    for s in range(1,longest):
        for j,ch in enumerate(chunks):
            if s<len(ch[5]): act(ch,s)
    for ci,i,lo,hi,both,routes in chunks:
        if not both: continue
        for (k,rx,ry),_ in routes:
            zz=lax.rem(z+nz-k,nz); xx=1-x if rx else x; yy=1-y if ry else y
            dst=block(i,lo,hi,zz,xx,yy,1-c,both)
            pltpu.make_async_remote_copy(dst,dst,send.at[0],recv.at[ci,yy*2+1-c,zz*2+xx],device_id=peer(pos,"c",nz),device_id_type=MESH).wait_recv()
    for cp in sent: cp.wait_send()
    for cp in locs: cp.wait()

def gather(shards,plan,dp,mp,cid,interp=False):
    nz=dp//2; n=len(shards)
    inside={i for i,_,_,o in plan if o=="zx"}
    outs=[jax.ShapeDtypeStruct(((dp,) if i in inside else (mp,dp))+s.shape,s.dtype) for i,s in enumerate(shards)]
    sends=sum(len(f) for _,_,_,o in plan for _,f in gather_routes(o,nz))
    return pl.pallas_call(functools.partial(gather_kernel,nz,plan,n),
        in_specs=[pl.BlockSpec(memory_space=pltpu.VMEM)]*n,
        out_specs=[pl.BlockSpec(memory_space=pl.ANY)]*n,
        out_shape=outs,
        scratch_shapes=[pltpu.SemaphoreType.DMA((sends,)),pltpu.SemaphoreType.DMA((len(plan),mp,dp)),pltpu.SemaphoreType.DMA((n,))],
        compiler_params=pltpu.CompilerParams(collective_id=cid,has_side_effects=True),name="gather_weights")(*shards)

def scatter_kernel(nz,plan,n,*refs):
    parts=refs[:n]; outs=refs[n:2*n]
    np_=len(plan)
    per=refs[2*n:2*n+5*np_]
    send,csem,xsem,ysem,zsem=refs[2*n+5*np_:]
    pos=coords(nz); z,x,y,c=pos
    kinds=[f"z{k}" for k in range(1,nz)]+["x","y","c"]
    greet(pos,kinds,nz)
    sent=[]
    def start(src,dst,rsem,kind):
        cp=pltpu.make_async_remote_copy(src,dst,send.at[len(sent)],rsem,device_id=peer(pos,kind,nz),device_id_type=MESH)
        cp.start(); sent.append(cp)
    def wait(dst,rsem):
        pltpu.make_async_remote_copy(dst,dst,send.at[0],rsem,device_id=peer(pos,"c",nz),device_id_type=MESH).wait_recv()
    def part(i,lo,hi,r,cc):
        rz,rx,ry=r
        zz=lax.rem(z+rz,nz); xx=1-x if rx else x; yy=1-y if ry else y
        if len(parts[i].shape)==4: return parts[i].at[yy*2+cc,zz*2+xx,:,lo:hi]
        return parts[i].at[zz*2+xx,:,lo:hi]
    def ordering(order):
        if order=="xyz":
            return [(k,1,r) for r in (1,0) for k in range(nz-1,-1,-1)]+[(k,0,1) for k in range(nz-1,-1,-1)]+[(k,0,0) for k in range(nz-1,-1,-1)]
        if order=="yzx":
            return [(k,r,1) for r in (1,0) for k in range(nz-1,-1,-1)]+[(k,1,0) for k in range(nz-1,-1,-1)]+[(k,0,0) for k in range(nz-1,-1,-1)]
        return [(k,1,0) for k in range(nz-1,-1,-1)]+[(k,0,0) for k in range(nz-1,-1,-1)]
    state=[]
    for p,(i,lo,hi,order) in enumerate(plan):
        acc,cb,xb,yb,zb=per[5*p:5*p+5]
        state.append((p,i,lo,hi,order,ordering(order),acc,cb,xb,yb,zb))
    def slot(order,r):
        return (r[0]*2+r[1])*2+r[2] if order!="xz" else r[0]*2+r[1]
    L=max(len(s[5]) for s in state)
    for t in range(L):
        for p,i,lo,hi,order,seq,acc,cb,xb,yb,zb in state:
            if t<len(seq):
                r=seq[t]; s=slot(order,r)
                start(part(i,lo,hi,r,1-c) if order!="xz" else part(i,lo,hi,r,c),cb.at[s],csem.at[p,s],"c")
    def add(acc_ref,*others):
        v=acc_ref[...].astype(f32)
        for o in others: v=v+o[...].astype(f32)
        return v
    def first_phase(st,t):
        p,i,lo,hi,order,seq,acc,cb,xb,yb,zb=st
        r=seq[t]; s=slot(order,r)
        wait(cb.at[s],csem.at[p,s])
        acc[s]=add(part(i,lo,hi,r,c),cb.at[s]).astype(bf)
        rz,rx,ry=r
        if order in ("xyz","xz") and rx: start(acc.at[s],xb.at[rz*2+ry],xsem.at[p,rz*2+ry],"x")
        if order=="yzx" and ry: start(acc.at[s],yb.at[rz*2+rx],ysem.at[p,rz*2+rx],"y")
    for t in range(L):
        for st in state:
            if t<len(st[5]): first_phase(st,t)
    def later(st):
        p,i,lo,hi,order,seq,acc,cb,xb,yb,zb=st
        A=lambda r: acc.at[slot(order,r)]
        if order=="xyz":
            for k in range(nz-1,-1,-1):
                r=(k,0,1); j=k*2+1
                wait(xb.at[j],xsem.at[p,j]); A(r)[...]=add(A(r),xb.at[j]).astype(bf)
                start(A(r),yb.at[k*2],ysem.at[p,k*2],"y")
            yield
            for k in range(nz-1,-1,-1):
                r=(k,0,0); j=k*2
                wait(xb.at[j],xsem.at[p,j]); wait(yb.at[k*2],ysem.at[p,k*2])
                if k:
                    A(r)[...]=add(A(r),xb.at[j],yb.at[k*2]).astype(bf)
                    start(A(r),zb.at[k],zsem.at[p,k],f"z{k}")
            yield
            for k in range(1,nz): wait(zb.at[k],zsem.at[p,k])
            outs[i][:,lo:hi]=add(A((0,0,0)),xb.at[0],yb.at[0],*[zb.at[k] for k in range(1,nz)])
        elif order=="yzx":
            for rx in (1,0):
                for k in range(nz-1,0,-1):
                    r=(k,rx,0); j=k*2+rx
                    wait(yb.at[j],ysem.at[p,j]); A(r)[...]=add(A(r),yb.at[j]).astype(bf)
                    start(A(r),zb.at[k*2+rx],zsem.at[p,k*2+rx],f"z{k}")
            yield
            r=(0,1,0)
            wait(yb.at[1],ysem.at[p,1])
            for k in range(1,nz): wait(zb.at[k*2+1],zsem.at[p,k*2+1])
            A(r)[...]=add(A(r),yb.at[1],*[zb.at[k*2+1] for k in range(1,nz)]).astype(bf)
            start(A(r),xb.at[0],xsem.at[p,0],"x")
            wait(yb.at[0],ysem.at[p,0])
            for k in range(1,nz): wait(zb.at[k*2],zsem.at[p,k*2])
            yield
            wait(xb.at[0],xsem.at[p,0])
            outs[i][:,lo:hi]=add(A((0,0,0)),yb.at[0],xb.at[0],*[zb.at[k*2] for k in range(1,nz)])
        else:
            for k in range(nz-1,-1,-1):
                r=(k,0,0); wait(xb.at[k*2],xsem.at[p,k*2]); A(r)[...]=add(A(r),xb.at[k*2]).astype(bf)
                start(A(r),yb.at[k],ysem.at[p,k],"y")
            yield
            for k in range(nz-1,0,-1):
                wait(yb.at[k],ysem.at[p,k]); zb[k]=add(A((k,0,0)),yb.at[k]).astype(bf)
                start(zb.at[k],zb.at[nz+k],zsem.at[p,k],f"z{k}")
            wait(yb.at[0],ysem.at[p,0])
            yield
            for k in range(1,nz): wait(zb.at[nz+k],zsem.at[p,k])
            outs[i][:,lo:hi]=add(A((0,0,0)),yb.at[0],*[zb.at[nz+k] for k in range(1,nz)])
    gens=[later(st) for st in state]
    live=list(gens)
    while live:
        nxt=[]
        for g in live:
            try: next(g); nxt.append(g)
            except StopIteration: pass
        live=nxt
    for cp in sent: cp.wait_send()

def scatter(parts,plan,dp,mp,cid):
    nz=dp//2; n=len(parts)
    outs=[jax.ShapeDtypeStruct(p.shape[-2:],f32) for p in parts]
    scr=[]; sends=0
    for i,lo,hi,order in plan:
        rows=parts[i].shape[-2]; w=hi-lo
        b=lambda k: pltpu.VMEM((k,rows,w),bf)
        nb=nz*4 if order!="xz" else nz*2
        scr+=[b(nb),b(nb)]
        if order=="xyz": scr+=[b(nz*2),b(nz*2),b(nz)]; sends+=nb+2*nz+nz+nz-1
        elif order=="yzx": scr+=[b(1),b(nz*2),b(nz*2)]; sends+=nb+2*nz+2*(nz-1)+1
        else: scr+=[b(nz*2),b(nz),b(2*nz)]; sends+=nb+nz+nz+nz-1
    np_=len(plan)
    return pl.pallas_call(functools.partial(scatter_kernel,nz,plan,n),
        in_specs=[pl.BlockSpec(memory_space=pltpu.VMEM)]*n,
        out_specs=[pl.BlockSpec(memory_space=pltpu.VMEM)]*n,
        out_shape=outs,
        scratch_shapes=scr+[pltpu.SemaphoreType.DMA((sends,)),pltpu.SemaphoreType.DMA((np_,4*nz)),pltpu.SemaphoreType.DMA((np_,2*nz)),pltpu.SemaphoreType.DMA((np_,2*nz)),pltpu.SemaphoreType.DMA((np_,2*nz))],
        compiler_params=pltpu.CompilerParams(collective_id=cid,has_side_effects=True,vmem_limit_bytes=60<<20),name="scatter_grads")(*parts)

NT=(((1,),(1,)),((),()))
NN=(((1,),(0,)),((),()))
def dg(a,b,dn): return lax.dot_general(a,b,dn,preferred_element_type=f32)
B=512
def attn_kernel(rb_ref,q_ref,do_ref,kv_ref,o_ref,dq_ref,dkv_ref,k2,v2,kvt,acck,accv,ps,mk):
    pair=pl.program_id(1)
    rb=rb_ref[0]
    nkb=kv_ref.shape[1]//B
    @pl.when(pair==0)
    def _():
        for kb in range(nkb):
            kv=kv_ref[0,kb*B:(kb+1)*B,:].astype(f32)
            rolled=pltpu.roll(kv,64,1)
            lane=lax.broadcasted_iota(jnp.int32,kv.shape,1)<64
            k2[kb]=jnp.where(lane,kv,rolled).astype(bf)
            v2[kb]=jnp.where(lane,rolled,kv).astype(bf)
            kvt[kb]=kv.T.astype(bf)
        acck[...]=jnp.zeros_like(acck); accv[...]=jnp.zeros_like(accv)
    q=q_ref[...]; do=do_ref[...]
    lane=lax.broadcasted_iota(jnp.int32,q.shape,1)<64
    zero=jnp.zeros_like(q)
    qm=(jnp.where(lane,q,zero),jnp.where(lane,zero,q))
    dom=(jnp.where(lane,do,zero),jnp.where(lane,zero,do))
    dot_=do.astype(f32).T
    def fwd(kb,carry,masked):
        new=[]
        for h in range(2):
            m,l,ot=carry[h]
            s=dg(k2[kb],qm[h],NT)
            if masked:
                ki=lax.broadcasted_iota(jnp.int32,s.shape,0); ri=lax.broadcasted_iota(jnp.int32,s.shape,1)
                s=jnp.where(ki<=ri,s,-1e30)
            mn=jnp.maximum(m,jnp.max(s,axis=0,keepdims=True))
            a=jnp.exp(m-mn)
            p=jnp.exp(s-mn)
            l=l*a+jnp.sum(p,axis=0,keepdims=True)
            pb=p.astype(bf)
            ps[h,kb]=pb
            mk[h,kb]=mn
            ot=ot*a+dg(kvt[kb,64:,:],pb,NN)
            new.append((mn,l,ot))
        return tuple(new)
    init=tuple((jnp.full((1,B),-1e30,f32),jnp.zeros((1,B),f32),jnp.zeros((64,B),f32)) for _ in range(2))
    carry=lax.fori_loop(0,rb,lambda kb,c: fwd(kb,c,False),init)
    carry=fwd(rb,carry,True)
    stats=[]
    ots=[]
    for h in range(2):
        m,l,ot=carry[h]
        inv=1.0/l
        ot=ot*inv
        ots.append(ot)
        delta=jnp.sum(ot*dot_[64*h:64*h+64,:],axis=0,keepdims=True)
        stats.append((m,inv,delta))
    o_ref[...]=jnp.concatenate(ots,axis=0).T.astype(bf)
    def bwd(kb,carry):
        new=[]; dsl=[]; pl_=[]
        for h in range(2):
            m,inv,delta=stats[h]
            alpha=jnp.exp(mk[h,kb]-m)*inv
            dp=dg(v2[kb],dom[h],NT)
            p=ps[h,kb].astype(f32)*alpha
            ds=(p*(dp-delta)).astype(bf)
            pn=p.astype(bf)
            acck[kb]+=dg(ds,qm[h],NN)
            accv[kb]+=dg(pn,dom[h],NN)
            new.append(carry[h]+dg(kvt[kb,:64,:],ds,NN))
        return tuple(new)
    c=lax.fori_loop(0,rb+1,bwd,(jnp.zeros((64,B),f32),jnp.zeros((64,B),f32)))
    dq_ref[...]=jnp.concatenate(c,axis=0).T
    @pl.when(pair==pl.num_programs(1)-1)
    def _():
        for kb in range(nkb):
            k=acck[kb]; v=accv[kb]
            lane=lax.broadcasted_iota(jnp.int32,k.shape,1)<64
            dkv_ref[0,kb*B:(kb+1)*B,:]=jnp.where(lane,k+pltpu.roll(k,64,1),v+pltpu.roll(v,64,1))
def attention(rb,q,do,kv,interpret=False):
    n=kv.shape[0]; S=kv.shape[1]; nkb=S//B
    blk=pl.BlockSpec((B,128),lambda b,p,r:(b,p))
    kvs=pl.BlockSpec((1,S,128),lambda b,p,r:(b,0,0))
    return pl.pallas_call(attn_kernel,
      grid_spec=pltpu.PrefetchScalarGridSpec(num_scalar_prefetch=1,grid=(n,6),in_specs=[blk,blk,kvs],out_specs=[blk,blk,kvs],
        scratch_shapes=[pltpu.VMEM((nkb,B,128),bf),pltpu.VMEM((nkb,B,128),bf),pltpu.VMEM((nkb,128,B),bf),pltpu.VMEM((nkb,B,128),f32),pltpu.VMEM((nkb,B,128),f32),
                        pltpu.VMEM((2,nkb,B,B),bf),pltpu.VMEM((2,nkb,1,B),f32)]),
      out_shape=[jax.ShapeDtypeStruct(q.shape,bf),jax.ShapeDtypeStruct(q.shape,f32),jax.ShapeDtypeStruct(kv.shape,f32)],
      compiler_params=pltpu.CompilerParams(vmem_limit_bytes=56<<20),name="attn")(rb,q,do,kv)


def kv_gather_kernel(nz, own_ref, full_ref, send, recv):
    pos = coords(nz)
    z, x, y, c = pos
    greet(pos, ["y", "c"], nz)
    nb = own_ref.shape[0]
    sent = []

    def go(b, m, src, kind):
        cp = pltpu.make_async_remote_copy(src, full_ref.at[b, m], send.at[len(sent)], recv.at[b, m],
                                          device_id=peer(pos, kind, nz), device_id_type=MESH)
        cp.start()
        sent.append(cp)

    def wait(b, m):
        pltpu.make_async_remote_copy(full_ref.at[b, m], full_ref.at[b, m], send.at[0], recv.at[b, m],
                                     device_id=peer(pos, "c", nz), device_id_type=MESH).wait_recv()

    for b in range(nb):
        go(b, y * 2 + c, own_ref.at[b], "y")
    for b in range(nb):
        go(b, y * 2 + c, own_ref.at[b], "c")
    for b in range(nb):
        full_ref[b, y * 2 + c] = own_ref[b]
    for b in range(nb):
        m = (1 - y) * 2 + c
        wait(b, m)
        go(b, m, full_ref.at[b, m], "c")
    for b in range(nb):
        wait(b, y * 2 + 1 - c)
        wait(b, (1 - y) * 2 + 1 - c)
    for cp in sent:
        cp.wait_send()


def kv_gather(own, dp, cid):
    nb, rows, w = own.shape
    return pl.pallas_call(
        functools.partial(kv_gather_kernel, dp // 2),
        in_specs=[pl.BlockSpec(memory_space=pltpu.VMEM)],
        out_specs=pl.BlockSpec(memory_space=pltpu.VMEM),
        out_shape=jax.ShapeDtypeStruct((nb, 4, rows, w), own.dtype),
        scratch_shapes=[pltpu.SemaphoreType.DMA((3 * nb,)), pltpu.SemaphoreType.DMA((nb, 4))],
        compiler_params=pltpu.CompilerParams(collective_id=cid, has_side_effects=True),
        name="gather_keyval",
    )(own)


def kv_reduce_kernel(nz, parts_ref, out_ref, low, cbuf, ybuf, ysend, send, crecv, yrecv):
    pos = coords(nz)
    z, x, y, c = pos
    greet(pos, ["y", "c"], nz)
    nb = parts_ref.shape[0]
    sent = []

    def go(src, dst, sem, kind):
        cp = pltpu.make_async_remote_copy(src, dst, send.at[len(sent)], sem, device_id=peer(pos, kind, nz), device_id_type=MESH)
        cp.start()
        sent.append(cp)

    def wait(dst, sem):
        pltpu.make_async_remote_copy(dst, dst, send.at[0], sem, device_id=peer(pos, "c", nz), device_id_type=MESH).wait_recv()

    for ry in (1, 0):
        yy = 1 - y if ry else y
        for b in range(nb):
            low[b, ry] = parts_ref[b, yy * 2 + 1 - c].astype(bf)
            go(low.at[b, ry], cbuf.at[b, ry], crecv.at[b, ry], "c")
    for b in range(nb):
        wait(cbuf.at[b, 1], crecv.at[b, 1])
        ysend[b] = (parts_ref[b, (1 - y) * 2 + c] + cbuf[b, 1].astype(f32)).astype(bf)
        go(ysend.at[b], ybuf.at[b], yrecv.at[b], "y")
    for b in range(nb):
        wait(cbuf.at[b, 0], crecv.at[b, 0])
        wait(ybuf.at[b], yrecv.at[b])
        out_ref[b] = parts_ref[b, y * 2 + c] + cbuf[b, 0].astype(f32) + ybuf[b].astype(f32)
    for cp in sent:
        cp.wait_send()


def kv_reduce(parts, dp, cid):
    nb, mp, rows, w = parts.shape
    return pl.pallas_call(
        functools.partial(kv_reduce_kernel, dp // 2),
        in_specs=[pl.BlockSpec(memory_space=pltpu.VMEM)],
        out_specs=pl.BlockSpec(memory_space=pltpu.VMEM),
        out_shape=jax.ShapeDtypeStruct((nb, rows, w), f32),
        scratch_shapes=[pltpu.VMEM((nb, 2, rows, w), bf), pltpu.VMEM((nb, 2, rows, w), bf), pltpu.VMEM((nb, rows, w), bf),
                        pltpu.VMEM((nb, rows, w), bf), pltpu.SemaphoreType.DMA((3 * nb,)), pltpu.SemaphoreType.DMA((nb, 2)), pltpu.SemaphoreType.DMA((nb,))],
        compiler_params=pltpu.CompilerParams(collective_id=cid, has_side_effects=True),
        name="reduce_keyval",
    )(parts)


def gather_all(qo, mlp, kvg, dp, mp):
    if dp == 8:
        plan = [(0, 0, 256, "zyx"), (0, 256, 384, "xzy"), (2, 0, 256, "zx"), (1, 0, 1024, "zyx"), (1, 1024, 1536, "xzy")]
        a, b, c = gather([qo, mlp, kvg], plan, dp, mp, 1)
    else:
        both = lambda s: lax.all_gather(s, ("dp", "mp")).reshape((dp, mp) + s.shape).transpose(1, 0, 2, 3)
        a, b, c = both(qo), both(mlp), lax.all_gather(kvg, "dp")
    return a.reshape(mp, -1, a.shape[-1]), b.reshape(mp, -1, b.shape[-1]), c.reshape(-1, c.shape[-1])


def scatter_all(qo, mlp, kvg, dp, mp):
    rows = kvg.shape[0] // dp
    cut = lambda p: p.reshape(p.shape[:-2] + (dp, rows, p.shape[-1]))
    if dp == 8:
        plan = [(0, 0, 256, "xyz"), (0, 256, 384, "yzx"), (2, 0, 256, "xz"), (1, 0, 1024, "xyz"), (1, 1024, 1536, "yzx")]
        return scatter([cut(qo), cut(mlp), cut(kvg)], plan, dp, mp, 2)
    both = lambda p: lax.psum_scatter(cut(p).transpose(1, 0, 2, 3).reshape((dp * mp, rows, p.shape[-1])).astype(f32), ("dp", "mp"), scatter_dimension=0)
    return both(qo), both(mlp), lax.psum(lax.psum_scatter(cut(kvg).astype(f32), "dp", scatter_dimension=0), "mp")


def rotary(position, width, heads):
    lane = jnp.arange(width, dtype=jnp.int32)
    inside = lane % HD
    frequency = 10000.0 ** (-2.0 * (inside % (ROT // 2)).astype(f32) / ROT)
    angle = position[:, None].astype(f32) * frequency[None, :]
    turned = ((inside < ROT) & (lane < heads * HD))[None, :]
    low = (inside < ROT // 2)[None, :]
    cosine = jnp.where(turned, jnp.cos(angle), 1.0)
    sine = jnp.where(turned, jnp.sin(angle), 0.0)
    return cosine, jnp.where(low, -sine, 0.0), jnp.where(low, 0.0, sine)


def rotate(v, tables, back=False):
    cosine, up, down = tables
    half = ROT // 2
    a = jnp.roll(v, -half, axis=1) * up
    b = jnp.roll(v, half, axis=1) * down
    return v * cosine - a - b if back else v * cosine + a + b


def shards(tokens, norm_gains, norm_biases, w_query, w_keyval, w_output, w_up, w_down, cotangent, subset_ids, subset_weights):
    dp, mp = lax.axis_size("dp"), lax.axis_size("mp")
    me = lax.axis_index("mp")
    nb, own, width = tokens.shape
    rows = nb * own
    heads = width // HD
    cols = w_query.shape[1]
    ff = w_up.shape[1]
    dot = functools.partial(jnp.dot, preferred_element_type=f32)
    nt = lambda a, b: lax.dot_general(a, b, (((1,), (1,)), ((), ())), preferred_element_type=f32)
    tn = lambda a, b: lax.dot_general(a, b, (((0,), (0,)), ((), ())), preferred_element_type=f32)
    qo = jnp.concatenate([w_query, w_output], axis=1)
    mlp = jnp.concatenate([w_up, w_down], axis=1)
    kvg = jnp.concatenate([w_keyval, norm_gains, norm_biases, jnp.zeros((w_keyval.shape[0], 124), bf)], axis=1)
    qo, mlp, kvg = gather_all(qo, mlp, kvg, dp, mp)
    wq = qo[:, :, :cols].transpose(1, 0, 2).reshape(width, width)
    wo = qo[:, :, cols:].transpose(1, 0, 2).reshape(width, width)
    wkv = kvg[:, : 2 * HD]
    small = kvg[:, 2 * HD : 2 * HD + 4].astype(f32).T
    gain_a, gain_m, bias_a, bias_m = small[0], small[1], small[2], small[3]

    ids = lax.dynamic_slice_in_dim(subset_ids.reshape(nb, mp * own), me * own, own, 1).reshape(rows)
    matches = ids[:, None] == jnp.arange(subset_weights.shape[0], dtype=jnp.int32)[None, :]
    scale = jnp.sum(jnp.where(matches, subset_weights[None, :], 0.0), axis=1, keepdims=True)
    grad_rows = cotangent.reshape(rows, width).astype(f32) * scale
    g = grad_rows.astype(bf)

    x = tokens.reshape(rows, width).astype(f32)
    centered = x - jnp.mean(x, axis=1, keepdims=True)
    inverse = lax.rsqrt(jnp.mean(centered * centered, axis=1, keepdims=True) + epsilon)
    normed = centered * inverse
    attn_in = (normed * gain_a + bias_a).astype(bf)
    mlp_in = (normed * gain_m + bias_m).astype(bf)
    position = jnp.tile(me * own + jnp.arange(own, dtype=jnp.int32), nb)
    tables = rotary(position, width, heads)
    kv_tables = rotary(position, 2 * HD, 1)
    q = (rotate(dot(attn_in, wq), tables) * HD ** (-0.5)).astype(bf)
    kv = rotate(dot(attn_in, wkv), kv_tables).astype(bf)
    kv_full = kv_gather(kv.reshape(nb, own, 2 * HD), dp, 3).reshape(nb, mp * own, 2 * HD)
    grad_heads = dot(g, wo).astype(bf)
    o, dq, dkv = attention(me.reshape(1), q, grad_heads, kv_full)
    dkv = kv_reduce(dkv.reshape(nb, mp, own, 2 * HD), dp, 4).reshape(rows, 2 * HD)

    out = x + nt(o, wo)
    dmlp = jnp.zeros((rows, width), f32)
    grads = []
    for m in range(mp):
        up, down = mlp[m, :, :ff], mlp[m, :, ff:]
        pre = dot(mlp_in, up)
        cdf = 0.5 * (1.0 + lax.erf(pre * sqrt_half))
        hidden = (pre * cdf).astype(bf)
        out = out + nt(hidden, down)
        slope = cdf + pre * (jnp.exp(-0.5 * pre * pre) * inv_sqrt_two_pi)
        dpre = (dot(g, down) * slope).astype(bf)
        dmlp = dmlp + nt(dpre, up)
        grads.append(jnp.concatenate([tn(mlp_in, dpre).astype(bf), tn(g, hidden).astype(bf)], axis=1))
    out = out.astype(bf)

    dqp = (rotate(dq, tables, True) * HD ** (-0.5)).astype(bf)
    dkvp = rotate(dkv, kv_tables, True).astype(bf)
    dattn = nt(dqp, wq) + nt(dkvp, wkv)
    dnormed = dattn * gain_a + dmlp * gain_m
    dx = (dnormed - jnp.mean(dnormed, axis=1, keepdims=True) - normed * jnp.mean(dnormed * normed, axis=1, keepdims=True)) * inverse
    input_grad = (grad_rows + dx).astype(bf)
    sums = jnp.stack([jnp.sum(dattn * normed, axis=0), jnp.sum(dmlp * normed, axis=0), jnp.sum(dattn, axis=0), jnp.sum(dmlp, axis=0)], axis=1)
    split = lambda a: a.astype(bf).reshape(width, mp, cols).transpose(1, 0, 2)
    gqo = jnp.concatenate([split(tn(attn_in, dqp)), split(tn(g, o))], axis=2)
    gkvg = jnp.concatenate([tn(attn_in, dkvp), sums, jnp.zeros((width, 124), f32)], axis=1).astype(bf)
    a, b, c = scatter_all(gqo, jnp.stack(grads), gkvg, dp, mp)
    k = 2 * HD
    return (
        out.reshape(tokens.shape),
        kv_full.reshape(-1, 2 * HD),
        input_grad.reshape(tokens.shape),
        c[:, k : k + 2],
        c[:, k + 2 : k + 4],
        a[:, :cols],
        c[:, :k],
        a[:, cols:],
        b[:, :ff],
        b[:, ff:],
    )


def solution(mesh):
    rows = P(None, ("dp", "mp"), None)
    d, dm = P("dp", None), P("dp", "mp")
    return jax.shard_map(
        shards,
        mesh=mesh,
        in_specs=(rows, d, d, dm, d, dm, dm, dm, rows, P("dp"), P()),
        out_specs=(rows, d, rows, d, d, dm, d, dm, dm, dm),
        check_vma=False,
    )
```

time: 1260 us -> 539 us (0.43)
  waiting for transfers between devices: 614 us -> 0 us
  Pallas kernels: 0 us -> 314 us
  matrix products: 304 us -> 89.4 us
  blocking collectives: 148 us -> 0 us
  other arithmetic: 135 us -> 65.9 us
  local copies, waits for them, and re-layouts: 32.3 us -> 62.7 us
  between operations: 17.6 us -> 1.67 us
    reduce_scatter x9 -> x0, waiting for transfers between devices: 579 us -> none  [the longest x2 120 us: shards(): lax.psum_scatter(branch_sum, 'mp', scatter_dimension=0, tiled=True)]
    pallas_call x0 -> x5, Pallas kernels: none -> 314 us  [the longest x1 102 us: kv_reduce(): pl.pallas_call(functools.partial(kv_reduce_kernel, dp // 2), in_specs=[pl...]
    dot_general x78 -> x33, matrix products: 304 us -> 89.4 us  [the longest x11 30.7 us: shards(): lax.dot_general(a, b, (((0,), (0,)), ((), ())), preferred_element_type=f32)]
    all_gather x5 -> x0, blocking collectives: 138 us -> none  [the longest x1 33.3 us: shards(): lax.all_gather(w_output, 'dp', axis=0, tiled=True)]
    another operation x20 -> x1, other arithmetic: 73.8 us -> 8.42 us  [shards(): a, b, c = scatter_all(gqo, jnp.stack(grads), gkvg, dp, mp)]
    convert_element_type x7 -> x8, other arithmetic: 5.33 us -> 41 us  [the longest x1 16.2 us: shards(): q = (rotate(dot(attn_in, wq), tables) * HD ** (-0.5)).astype(bf)]
    unnamed x20 -> x0, waiting for transfers between devices: 34.2 us -> none
    concatenate x2 -> x10, local copies, waits for them, and re-layouts: 1.41 us -> 24.1 us  [the longest x4 17.1 us: shards(): jnp.concatenate([tn(mlp_in, dpre).astype(bf), tn(g, hidden).astype(bf)],...]
  transfers between devices with their start and end apart: 18 -> 0, of which waited for: 10 -> 0; matrix products, arithmetic and copies ran while one was open for 35% -> 0% of each run, Pallas kernels for 0% -> 0%
where the time goes in v1:
time: 539 us; the launch traced here: 533 us
  Pallas kernels  314 us (58%)
  matrix products  89.4 us (17%)
  other arithmetic  65.9 us (12%)
  local copies, waits for them, and re-layouts  62.7 us (12%)
    pallas_call x1, Pallas kernels, kv_reduce(): pl.pallas_call(functools.partial(kv_reduce_kernel, dp // 2), in_specs=[pl...  102 us
    pallas_call x1, Pallas kernels, scatter(): pl.pallas_call(functools.partial(scatter_kernel, nz, plan, n), in_specs=[...  91.4 us
    pallas_call x1, Pallas kernels, gather(): pl.pallas_call(functools.partial(gather_kernel, nz, plan, n), in_specs=[p...  71.5 us
    pallas_call x1, Pallas kernels, attention(): pl.pallas_call(attn_kernel, grid_spec=pltpu.PrefetchScalarGridSpec(num_sc...  35.8 us
    dot_general x11, matrix products, shards(): lax.dot_general(a, b, (((0,), (0,)), ((), ())), preferred_element_type=f32)  30.7 us
    dot_general x11, matrix products, shards(): lax.dot_general(a, b, (((1,), (1,)), ((), ())), preferred_element_type=f32)  29.7 us
    concatenate x4, local copies, waits for them, and re-layouts, shards(): jnp.concatenate([tn(mlp_in, dpre).astype(bf), tn(g, hidden).astype(bf)],...  17.1 us
    convert_element_type x1, other arithmetic, shards(): q = (rotate(dot(attn_in, wq), tables) * HD ** (-0.5)).astype(bf)  16.2 us

profile of v1, /device:TPU:0, one launch (start us, length us, event | category | flops | bytes accessed | tf_op | source)
XLA Modules:
  0.0 533.3 jit_solution(17702741956945602609)
XLA Ops:
  7.1 71.5 %gather_weights.1 = (bf16[4,8,96,384]{3,2,1,0:T(8,128)(2,1)}, bf16[4,8,96,1536]{3,2,1,0:T(8,128)(2,1)}, bf16[8,96,256]{2,1,0:T(8,128)(2,1)}) custom-call(bf16[96,384]{1,0:T(8,128)(2,1)} %pad_maximum_fusion.7.refs_0_, bf16[96,1536]{1,0:T(8,128)(2,1)} %pad_maximum_fusion.6.refs_1_, bf16[96,256]{1,0:T(8,128)(2,1)} %maximum_maximum_fusion.refs_2_), custom_call_target="tpu_custom_call" | custom-call | tf_op jit(solution)/shard_map/gather_weights/pallas_call | solution.py:110
  85.2 2.9 copy.116
  88.1 3.2 fusion.170
  91.3 3.6 fusion.161
  96.1 16.2 %fusion.6.q_ref = bf16[1024,768]{1,0:T(8,128)(2,1)} fusion(f32[1024,768]{1,0:T(8,128)} %copy-done.2, f32[1024,8]{1,0:T(8,128)} %get-tuple-element.79, f32[1024,760]{1,0:T(8,128)} %get-tuple-element.81, f32[1024,760]{1,0:T(8,128)} %get-tuple-element.80, f32[1024,8]{1,0:T(8,128)} %get-tuple-element.78, f32[768]{0:T(1024)S(1)} %fusion.140, ...), kind=kLoop, calls=%fused_computation.13 | loop fusion | flops 11796480 | bytes 11018752 | tf_op jit(solution)/shard_map/convert_element_type | solution.py:503
  118.3 13.1 %gather_keyval.1 = bf16[2,4,512,128]{3,2,1,0:T(8,128)(2,1)} custom-call(bf16[2,512,128]{2,1,0:T(8,128)(2,1)} %bitcast.220), custom_call_target="tpu_custom_call" | custom-call | tf_op jit(solution)/shard_map/gather_keyval/pallas_call | solution.py:370
  131.6 2.9 multiply_convert_fusion.4
  136.0 4.3 convolution_convert_fusion.do_ref
  140.3 35.8 %attn.1 = (bf16[1024,768]{1,0:T(8,128)(2,1)}, f32[1024,768]{1,0:T(8,128)}, f32[2,2048,128]{2,1,0:T(8,128)}) custom-call(s32[1]{0:T(128)} %bitcast.1.rb_ref, bf16[1024,768]{1,0:T(8,128)(2,1)} %fusion.6.q_ref, bf16[1024,768]{1,0:T(8,128)(2,1)} %convolution_convert_fusion.do_ref, bf16[2,2048,128]{2,1,0:T(8,128)(2,1)} %bitcast.194), custom_call_target="tpu_custom_call" | custom-call | tf_op jit(solution)/shard_map/attn/pallas_call | solution.py:326
  176.1 101.8 %reduce_keyval.1 = f32[2,512,128]{2,1,0:T(8,128)} custom-call(f32[2,4,512,128]{3,2,1,0:T(8,128)} %bitcast.200), custom_call_target="tpu_custom_call" | custom-call | tf_op jit(solution)/shard_map/reduce_keyval/pallas_call | solution.py:415
  283.3 4.5 fusion.76
  289.0 13.4 %fusion.10 = bf16[1024,768]{1,0:T(8,128)(2,1)S(1)} fusion(f32[1024,768]{1,0:T(8,128)S(1)} %copy-done.1, f32[1024,8]{1,0:T(8,128)S(1)} %get-tuple-element.75, f32[1024,760]{1,0:T(8,128)S(1)} %get-tuple-element.77, f32[1024,760]{1,0:T(8,128)S(1)} %get-tuple-element.76, f32[1024,8]{1,0:T(8,128)S(1)} %get-tuple-element.74, f32[768]{0:T(1024)S(1)} %fusion.140, ...), kind=kLoop, calls=%fused_computation.17 | loop fusion | flops 11796480 | bytes 11018752 | tf_op jit(solution)/shard_map/convert_element_type | solution.py:525
  306.5 3.0 multiply_convert_fusion.3
  313.6 3.0 multiply_convert_fusion.2
  320.8 2.9 multiply_convert_fusion.1
  333.5 5.6 %fusion.155 = (bf16[768]{0:T(1024)(128)(2,1)}, bf16[768]{0:T(1024)(128)(2,1)}, f32[1024]{0:T(1024)}, f32[1024]{0:T(1024)S(1)}, f32[1024,768]{1,0:T(8,128)}, /*in...) fusion(f32[1024]{0:T(1024)S(1)} %bitcast.252, f32[1024]{0:T(1024)S(1)} %bitcast.255, ...), kind=kOutput, calls=%fused_computation.236 | convolution fusion | flops 1224469504 | bytes 21661696 | tf_op jit(solution)/shard_map/dot_general | solution.py:476
  346.8 3.5 convolution_convert_fusion.8
  357.2 4.3 copy.98
  361.5 3.5 convolution_convert_fusion.6
  368.1 4.3 copy.99
  372.3 3.5 convolution_convert_fusion.4
  378.9 4.3 copy.100
  383.2 3.0 convolution_convert_fusion.2
  389.6 4.3 copy.101
  393.9 8.4 %pad_maximum_fusion.refs_1_ = bf16[4,8,96,1536]{3,2,1,0:T(8,128)(2,1)} fusion(bf16[1,8,96,1536]{3,2,1,0:T(8,128)(2,1)} %bitcast.193, bf16[1,8,96,1536]{3,2,1,0:T(8,128)(2,1)} %bitcast.192, bf16[1,8,96,1536]{3,2,1,0:T(8,128)(2,1)} %bitcast.191, bf16[1,8,96,1536]{3,2,1,0:T(8,128)(2,1)} %bitcast.190), kind=kLoop, calls=%fused_computation | loop fusion | flops 14155776 | bytes 18874368 | tf_op jit(solution)/shard_map/stack | solution.py:535
  407.4 3.9 convolution_convert_fusion.10
  413.9 3.6 pad_maximum_fusion.1
  417.6 91.4 %scatter_grads.1 = (f32[96,384]{1,0:T(8,128)}, f32[96,1536]{1,0:T(8,128)}, f32[96,256]{1,0:T(8,128)}) custom-call(bf16[4,8,96,384]{3,2,1,0:T(8,128)(2,1)} %bitcast.196, bf16[4,8,96,1536]{3,2,1,0:T(8,128)(2,1)} %pad_maximum_fusion.refs_1_, bf16[8,96,256]{2,1,0:T(8,128)(2,1)} %concatenate.109.refs_2_), custom_call_target="tpu_custom_call" | custom-call | tf_op jit(solution)/shard_map/scatter_grads/pallas_call | solution.py:239
  516.2 2.9 fusion.171
  522.0 2.8 fusion.82
  524.8 2.9 fusion.85
  527.7 4.4 fusion.74
  (168 shorter events, 92.9 us)
Async XLA Ops:
  0.6 79.1 %copy-start = (bf16[2,512,768]{2,1,0:T(8,128)(2,1)S(1)}, bf16[2,512,768]{2,1,0:T(8,128)(2,1)}, u32[]{:S(2)}) copy-start(bf16[2,512,768]{2,1,0:T(8,128)(2,1)} %param.11) | copy-start | bytes 4718596
  80.1 3.2 copy-start.9
  91.3 3.7 copy-start.2
  114.8 16.6 %copy-start.26 = (s32[4096]{0:T(1024)S(1)}, s32[4096]{0:T(1024)}, u32[]{:S(2)}) copy-start(s32[4096]{0:T(1024)} %param.20) | copy-start | bytes 49156
  114.8 16.7 %copy-start.27 = (f32[22]{0:T(128)S(1)}, f32[22]{0:T(128)}, u32[]{:S(2)}) copy-start(f32[22]{0:T(128)} %param.21) | copy-start | bytes 268
  283.2 4.5 copy-start.1
  288.9 13.5 %copy-start.22 = (bf16[4,768,192]{1,2,0:T(8,128)(2,1)S(1)}, bf16[4,768,192]{1,2,0:T(8,128)(2,1)}, u32[]{:S(2)}) copy-start(bf16[4,768,192]{1,2,0:T(8,128)(2,1)} %copy.116) | copy-start | bytes 3538948
  288.9 17.5 %slice-start = ((s8[9437184]{0:T(1024)(128)(4,1)}), s8[4194304]{0:T(1024)(128)(4,1)S(1)}, s32[]{:S(2)}) async-start(s8[9437184]{0:T(1024)(128)(4,1)} %bitcast.228), calls=%async_computation | async-start | bytes 8388608
  289.0 17.5 %slice-start.1 = ((s8[9437184]{0:T(1024)(128)(4,1)}), s8[4194304]{0:T(1024)(128)(4,1)S(1)}, s32[]{:S(2)}) async-start(s8[9437184]{0:T(1024)(128)(4,1)} %bitcast.228), calls=%async_computation.1 | async-start | bytes 8388608
  302.4 4.1 slice-start.2
  303.9 2.7 copy-start.14
  306.5 3.0 copy-start.13
  346.8 3.5 copy-start.25
  346.8 3.5 copy-start.3
  346.8 3.5 copy-start.8
  350.3 3.9 copy-start.29
  361.5 3.5 copy-start.17
  361.5 3.5 copy-start.31
  372.3 3.5 copy-start.18
  372.3 3.5 copy-start.33
  383.2 3.0 copy-start.11
  383.2 3.0 copy-start.19
  393.9 8.4 %copy-start.20 = (bf16[1024,768]{1,0:T(8,128)(2,1)S(1)}, bf16[1024,768]{1,0:T(8,128)(2,1)}, u32[]{:S(2)}) copy-start(bf16[1024,768]{1,0:T(8,128)(2,1)} %copy-done.16) | copy-start | bytes 4718596
  393.9 8.4 %copy-start.28 = (bf16[1024,768]{1,0:T(8,128)(2,1)S(1)}, bf16[1024,768]{1,0:T(8,128)(2,1)}, u32[]{:S(2)}) copy-start(bf16[1024,768]{1,0:T(8,128)(2,1)} %get-tuple-element.21) | copy-start | bytes 4718596
  402.3 5.1 copy-start.6
  411.3 2.6 copy-start.7
  417.6 98.7 %copy-start.21 = (bf16[4,768,192]{1,2,0:T(8,128)(2,1)S(1)}, bf16[4,768,192]{1,2,0:T(8,128)(2,1)}, u32[]{:S(2)}) copy-start(bf16[4,768,192]{1,2,0:T(8,128)(2,1)} %copy.117) | copy-start | bytes 3538948
  516.2 2.9 copy-start.30
  519.2 2.8 copy-start.32
  522.0 2.8 copy-start.34
  524.8 2.9 copy-start.12
  527.7 4.5 copy-start.4
  (9 other events, 12.9 us)

commit v2 on v1

v2 whole, which is shorter than its diff:
```python
import functools

import jax
import jax.numpy as jnp
from jax import lax
from jax.experimental import pallas as pl
from jax.experimental.pallas import tpu as pltpu
from jax.sharding import PartitionSpec as P

f32 = jnp.float32
bf = jnp.bfloat16
MESH = pl.DeviceIdType.MESH
HD = 64
ROT = 16
SEQ_LEN = 2048
epsilon = 1e-05
sqrt_half = 0.7071067811865476
inv_sqrt_two_pi = 0.3989422804014327


def coords(nz):
    d=lax.axis_index("dp"); m=lax.axis_index("mp")
    return d//2, d%2, m//2, m%2

def peer(pos,kind,nz):
    z,x,y,c=pos
    if kind[0]=="z": z=lax.rem(z+int(kind[1:]),nz)
    if kind=="x": x=1-x
    if kind=="y": y=1-y
    if kind=="c": c=1-c
    return (z*2+x, y*2+c)

def greet(pos,kinds,nz):
    bar=pltpu.get_barrier_semaphore()
    for k in kinds:
        pl.semaphore_signal(bar,inc=1,device_id=peer(pos,k,nz),device_id_type=MESH)
    pl.semaphore_wait(bar,len(kinds))

def gather_routes(order,nz):
    zs=[f"z{k}" for k in range(1,nz)]
    out=[]
    if order=="zyx":
        out.append(((0,0,0),zs+["y","x","c"]))
        out+=[((k,0,0),["y","x","c"]) for k in range(1,nz)]
        out+=[((k,0,1),["x","c"]) for k in range(nz)]
        out+=[((k,1,r),["c"]) for r in (0,1) for k in range(nz)]
    elif order=="xzy":
        out.append(((0,0,0),["x"]+zs+["y","c"]))
        out.append(((0,1,0),zs+["y","c"]))
        out+=[((k,r,0),["y","c"]) for k in range(1,nz) for r in (0,1)]
        out+=[((k,r,1),["c"]) for k in range(nz) for r in (0,1)]
    elif order=="zx":
        out.append(((0,0,0),zs+["x"]))
        out+=[((k,0,0),["x"]) for k in range(1,nz)]
        out+=[((k,1,0),[]) for k in range(nz)]
    return out

def columns(m,w,lo,hi):
    return pl.ds(pl.multiple_of(m*w+lo,128),hi-lo)

class Gather:
    def __init__(self,shards,plan,dp,mp):
        self.plan=plan; self.nz=dp//2; self.mp=mp; self.dp=dp
        inside={i for i,_,_,o in plan if o=="zx"}
        self.ins=[pl.BlockSpec(memory_space=pltpu.VMEM)]*len(shards)
        self.outs=[pl.BlockSpec(memory_space=pl.ANY)]*len(shards)
        self.shapes=[jax.ShapeDtypeStruct((dp,s.shape[0],s.shape[1]*(1 if i in inside else mp)),s.dtype) for i,s in enumerate(shards)]
        sends=sum(len(f) for _,_,_,o in plan for _,f in gather_routes(o,self.nz))
        self.scratch=[pltpu.SemaphoreType.DMA((sends,)),pltpu.SemaphoreType.DMA((len(plan),mp,dp)),pltpu.SemaphoreType.DMA((len(shards),))]
    def build(self,pos,shards,full,scr):
        send,recv,local=scr
        nz=self.nz; z,x,y,c=pos
        routes=[gather_routes(o,nz) for _,_,_,o in self.plan]
        sent=[]
        def where(p,rel,other):
            i,lo,hi,order=self.plan[p]; k,rx,ry=rel
            zz=lax.rem(z+nz-k,nz); xx=1-x if rx else x; yy=1-y if ry else y
            d=zz*2+xx; m=yy*2+(1-c if other else c)
            if order=="zx": return full[i].at[d,:,lo:hi],recv.at[p,0,d]
            return full[i].at[d,:,columns(m,shards[i].shape[1],lo,hi)],recv.at[p,m,d]
        def arrived(p,rel,other):
            dst,sem=where(p,rel,other)
            pltpu.make_async_remote_copy(dst,dst,send.at[0],sem,device_id=peer(pos,"c",nz),device_id_type=MESH).wait_recv()
        def copy(p,rel,f,own,n):
            i,lo,hi,_=self.plan[p]
            dst,sem=where(p,rel,False)
            src=shards[i].at[:,lo:hi] if own else dst
            return pltpu.make_async_remote_copy(src,dst,send.at[n],sem,device_id=peer(pos,f,nz),device_id_type=MESH)
        def step(p,s):
            rel,fw=routes[p][s]
            base=len(sent)
            cps=[functools.partial(copy,p,rel,f,s==0,base+j) for j,f in enumerate(fw)]
            sent.extend(cps)
            def go():
                if s: arrived(p,rel,False)
                for cp in cps: cp().start()
            return go
        def mine(i):
            order=[o for j,_,_,o in self.plan if j==i][0]
            d=z*2+x; w=shards[i].shape[1]
            dst=full[i].at[d] if order=="zx" else full[i].at[d,:,columns(y*2+c,w,0,w)]
            return pltpu.make_async_copy(shards[i],dst,local.at[i])
        first=[step(p,0) for p in range(len(self.plan))]
        steps=[]
        longest=max(len(r) for r in routes)
        for s in range(1,longest):
            for p,r in enumerate(routes):
                if s<len(r): steps.append(((s-1)/(longest-1),step(p,s)))
        def begin():
            for g in first: g()
            for i in range(len(shards)): mine(i).start()
        def end():
            for p,r in enumerate(routes):
                if self.plan[p][3]=="zx": continue
                for rel,_ in r: arrived(p,rel,True)
            for cp in sent: cp().wait_send()
            for i in range(len(shards)): mine(i).wait()
        return begin,steps,end

class Scatter:
    def __init__(self,parts,plan,dp,mp):
        self.plan=plan; nz=self.nz=dp//2; self.mp=mp
        self.width=[]
        for i,p in enumerate(parts):
            inside=[o for j,_,_,o in plan if j==i][0]=="xz"
            self.width.append(p.shape[-1]//(1 if inside else mp))
        self.ins=[pl.BlockSpec(memory_space=pltpu.VMEM)]*len(parts)
        self.outs=[pl.BlockSpec(memory_space=pltpu.VMEM)]*len(parts)
        self.shapes=[jax.ShapeDtypeStruct((p.shape[1],w),f32) for p,w in zip(parts,self.width)]
        scr=[]; sends=0
        for i,lo,hi,order in plan:
            rows=parts[i].shape[1]; w=hi-lo
            b=lambda k: pltpu.VMEM((k,rows,w),bf)
            nb=nz*4 if order!="xz" else nz*2
            scr+=[b(nb),b(nb)]
            if order=="xyz": scr+=[b(nz*2),b(nz),b(nz)]; sends+=nb+2*nz+nz+nz-1
            elif order=="yzx": scr+=[b(1),b(nz*2),b(nz*2)]; sends+=nb+2*nz+2*(nz-1)+1
            else: scr+=[b(nz*2),b(nz),b(2*nz)]; sends+=nb+nz+nz+nz-1
        n=len(plan)
        self.scratch=scr+[pltpu.SemaphoreType.DMA((sends,)),pltpu.SemaphoreType.DMA((n,4*nz)),pltpu.SemaphoreType.DMA((n,2*nz)),pltpu.SemaphoreType.DMA((n,2*nz)),pltpu.SemaphoreType.DMA((n,2*nz))]
    def build(self,pos,parts,outs,scr):
        plan=self.plan; nz=self.nz; z,x,y,c=pos; n=len(plan)
        per=scr[:5*n]; send,csem,xsem,ysem,zsem=scr[5*n:]
        sent=[]; begins=[]; steps=[]; ends=[]
        def sender(src,dst,rsem,kind):
            k=len(sent)
            cp=lambda: pltpu.make_async_remote_copy(src(),dst,send.at[k],rsem,device_id=peer(pos,kind,nz),device_id_type=MESH)
            sent.append(cp)
            return lambda: cp().start()
        def wait(dst,rsem):
            pltpu.make_async_remote_copy(dst,dst,send.at[0],rsem,device_id=peer(pos,"c",nz),device_id_type=MESH).wait_recv()
        def part(p,r,cc):
            i,lo,hi,order=plan[p]
            rz,rx,ry=r
            zz=lax.rem(z+rz,nz); xx=1-x if rx else x; yy=1-y if ry else y
            if order=="xz": return parts[i].at[zz*2+xx,:,lo:hi]
            return parts[i].at[zz*2+xx,:,columns(yy*2+cc,self.width[i],lo,hi)]
        def add(first,*others):
            v=first[...].astype(f32)
            for o in others: v=v+o[...].astype(f32)
            return v
        down=range(nz-1,-1,-1)
        for p,(i,lo,hi,order) in enumerate(plan):
            acc,cb,xb,yb,zb=per[5*p:5*p+5]
            if order=="xyz": seq=[(k,1,r) for r in (1,0) for k in down]+[(k,0,1) for k in down]+[(k,0,0) for k in down]
            elif order=="yzx": seq=[(k,r,1) for r in (1,0) for k in down]+[(k,1,0) for k in down]+[(k,0,0) for k in down]
            else: seq=[(k,1,0) for k in down]+[(k,0,0) for k in down]
            slot=(lambda r: (r[0]*2+r[1])*2+r[2]) if order!="xz" else (lambda r: r[0]*2+r[1])
            A=lambda r,acc=acc,slot=slot: acc.at[slot(r)]
            def plus(when,p=p):
                def note(f): steps.append((when,f))
                return note
            for t,r in enumerate(seq):
                s=slot(r); rz,rx,ry=r
                begins.append((t,sender(functools.partial(part,p,r,c if order=="xz" else 1-c),cb.at[s],csem.at[p,s],"c")))
                go=None
                if order in ("xyz","xz") and rx: go=sender(lambda v=A(r): v,xb.at[rz*2+ry],xsem.at[p,rz*2+ry],"x")
                if order=="yzx" and ry: go=sender(lambda v=A(r): v,yb.at[rz*2+rx],ysem.at[p,rz*2+rx],"y")
                @plus(0.22*t/len(seq))
                def _(p=p,r=r,s=s,acc=acc,cb=cb,go=go):
                    wait(cb.at[s],csem.at[p,s])
                    acc[s]=add(part(p,r,c),cb.at[s]).astype(bf)
                    if go: go()
            if order=="xyz":
                for n_,k in enumerate(down):
                    r=(k,0,1); j=k*2+1
                    go=sender(lambda v=A(r): v,yb.at[k],ysem.at[p,k],"y")
                    @plus(0.24+0.26*n_/nz)
                    def _(p=p,r=r,j=j,A=A,xb=xb,go=go):
                        wait(xb.at[j],xsem.at[p,j]); A(r)[...]=add(A(r),xb.at[j]).astype(bf)
                        go()
                for n_,k in enumerate(down):
                    r=(k,0,0); j=k*2
                    go=sender(lambda v=A(r): v,zb.at[k],zsem.at[p,k],f"z{k}") if k else None
                    @plus(0.52+0.26*n_/nz)
                    def _(p=p,r=r,j=j,k=k,A=A,xb=xb,yb=yb,go=go):
                        wait(xb.at[j],xsem.at[p,j]); wait(yb.at[k],ysem.at[p,k])
                        if go:
                            A(r)[...]=add(A(r),xb.at[j],yb.at[k]).astype(bf)
                            go()
                def fin(p=p,i=i,lo=lo,hi=hi,A=A,xb=xb,yb=yb,zb=zb):
                    for k in range(1,nz): wait(zb.at[k],zsem.at[p,k])
                    outs[i][:,lo:hi]=add(A((0,0,0)),xb.at[0],yb.at[0],*[zb.at[k] for k in range(1,nz)])
                ends.append(fin)
            elif order=="yzx":
                for n_,(rx,k) in enumerate([(rx,k) for rx in (1,0) for k in range(nz-1,0,-1)]):
                    r=(k,rx,0); j=k*2+rx
                    go=sender(lambda v=A(r): v,zb.at[k*2+rx],zsem.at[p,k*2+rx],f"z{k}")
                    @plus(0.24+0.3*n_/(2*nz-2))
                    def _(p=p,r=r,j=j,A=A,yb=yb,go=go):
                        wait(yb.at[j],ysem.at[p,j]); A(r)[...]=add(A(r),yb.at[j]).astype(bf)
                        go()
                r=(0,1,0)
                go=sender(lambda v=A(r): v,xb.at[0],xsem.at[p,0],"x")
                @plus(0.8)
                def _(p=p,r=r,A=A,yb=yb,zb=zb,go=go):
                    wait(yb.at[1],ysem.at[p,1])
                    for k in range(1,nz): wait(zb.at[k*2+1],zsem.at[p,k*2+1])
                    A(r)[...]=add(A(r),yb.at[1],*[zb.at[k*2+1] for k in range(1,nz)]).astype(bf)
                    go()
                def fin(p=p,i=i,lo=lo,hi=hi,A=A,xb=xb,yb=yb,zb=zb):
                    wait(yb.at[0],ysem.at[p,0])
                    for k in range(1,nz): wait(zb.at[k*2],zsem.at[p,k*2])
                    wait(xb.at[0],xsem.at[p,0])
                    outs[i][:,lo:hi]=add(A((0,0,0)),yb.at[0],xb.at[0],*[zb.at[k*2] for k in range(1,nz)])
                ends.append(fin)
            else:
                for n_,k in enumerate(down):
                    r=(k,0,0)
                    go=sender(lambda v=A(r): v,yb.at[k],ysem.at[p,k],"y")
                    @plus(0.24+0.26*n_/nz)
                    def _(p=p,r=r,k=k,A=A,xb=xb,go=go):
                        wait(xb.at[k*2],xsem.at[p,k*2]); A(r)[...]=add(A(r),xb.at[k*2]).astype(bf)
                        go()
                for n_,k in enumerate(range(nz-1,0,-1)):
                    go=sender(lambda v=zb.at[k]: v,zb.at[nz+k],zsem.at[p,k],f"z{k}")
                    @plus(0.52+0.26*n_/nz)
                    def _(p=p,k=k,A=A,yb=yb,zb=zb,go=go):
                        wait(yb.at[k],ysem.at[p,k]); zb[k]=add(A((k,0,0)),yb.at[k]).astype(bf)
                        go()
                def fin(p=p,i=i,lo=lo,hi=hi,A=A,yb=yb,zb=zb):
                    wait(yb.at[0],ysem.at[p,0])
                    for k in range(1,nz): wait(zb.at[nz+k],zsem.at[p,k])
                    outs[i][:,lo:hi]=add(A((0,0,0)),yb.at[0],*[zb.at[nz+k] for k in range(1,nz)])
                ends.append(fin)
        begins.sort(key=lambda e: e[0])
        steps.sort(key=lambda e: e[0])
        def begin():
            for _,g in begins: g()
        def end():
            for f in ends: f()
            for cp in sent: cp().wait_send()
        return begin,steps,end

def comm_kernel(nz,comm,n,*refs):
    pos=coords(nz)
    greet(pos,[f"z{k}" for k in range(1,nz)]+["x","y","c"],nz)
    begin,steps,end=comm.build(pos,refs[:n],refs[n:2*n],refs[2*n:])
    begin()
    for _,s in steps: s()
    end()

def communicate(comm,arrays,cid,name):
    return pl.pallas_call(functools.partial(comm_kernel,comm.nz,comm,len(arrays)),
        in_specs=comm.ins,out_specs=comm.outs,out_shape=comm.shapes,scratch_shapes=comm.scratch,
        compiler_params=pltpu.CompilerParams(collective_id=cid,has_side_effects=True,vmem_limit_bytes=60<<20),name=name)(*arrays)

NT=(((1,),(1,)),((),()))
NN=(((1,),(0,)),((),()))
def dg(a,b,dn): return lax.dot_general(a,b,dn,preferred_element_type=f32)
B=512
def turn(v,tab_ref,back):
    a=pltpu.roll(v,128-ROT//2,1)*tab_ref[1]
    b=pltpu.roll(v,ROT//2,1)*tab_ref[2]
    return v*tab_ref[0]-a-b if back else v*tab_ref[0]+a+b

def attn_kernel(nz,pairs,comm,nc,*refs):
    q_ref,do_ref,kv_ref,tab_ref=refs[:4]
    cin=refs[4:4+nc]
    o_ref,dq_ref,dkv_ref=refs[4+nc:7+nc]
    cout=refs[7+nc:7+2*nc]
    k2,v2,kvt,acck,accv,ps,mk,ms,ls,ots,dqs=refs[7+2*nc:18+2*nc]
    rb=lax.axis_index("mp")
    nkb=kv_ref.shape[1]//B
    slots=[[] for _ in range(pairs*2*nkb)]
    if comm:
        pos=coords(nz)
        greet(pos,[f"z{k}" for k in range(1,nz)]+["x","y","c"],nz)
        begin,steps,end=comm.build(pos,cin,cout,refs[18+2*nc:])
        begin()
        for when,s in steps: slots[int(when*len(slots))].append(s)
    def between(pair,kb,base):
        for p in range(pairs):
            todo=[k for k in range(nkb) if slots[(2*p+base)*nkb+k]]
            if not todo: continue
            @pl.when(pair==p)
            def _(p=p,todo=todo):
                for k in todo:
                    @pl.when(kb==k)
                    def _(k=k):
                        for s in slots[(2*p+base)*nkb+k]: s()
    for kb in range(nkb):
        kv=kv_ref[0,kb*B:(kb+1)*B,:].astype(f32)
        rolled=pltpu.roll(kv,64,1)
        lane=lax.broadcasted_iota(jnp.int32,kv.shape,1)<64
        k2[kb]=jnp.where(lane,kv,rolled).astype(bf)
        v2[kb]=jnp.where(lane,rolled,kv).astype(bf)
        kvt[kb]=kv.T.astype(bf)
    acck[...]=jnp.zeros_like(acck); accv[...]=jnp.zeros_like(accv)
    def one(pair,carry):
        cols=pl.ds(pl.multiple_of(pair*128,128),128)
        q=(turn(q_ref[:,cols],tab_ref,False)*HD**-0.5).astype(bf); do=do_ref[:,cols]
        lane=lax.broadcasted_iota(jnp.int32,q.shape,1)<64
        zero=jnp.zeros_like(q)
        qm=(jnp.where(lane,q,zero),jnp.where(lane,zero,q))
        dom=(jnp.where(lane,do,zero),jnp.where(lane,zero,do))
        ms[...]=jnp.full_like(ms,-1e30); ls[...]=jnp.zeros_like(ls)
        ots[...]=jnp.zeros_like(ots); dqs[...]=jnp.zeros_like(dqs)
        def fwd(kb,masked):
            for h in range(2):
                m=ms[h]
                s=dg(k2[kb],qm[h],NT)
                if masked:
                    ki=lax.broadcasted_iota(jnp.int32,s.shape,0); ri=lax.broadcasted_iota(jnp.int32,s.shape,1)
                    s=jnp.where(ki<=ri,s,-1e30)
                mn=jnp.maximum(m,jnp.max(s,axis=0,keepdims=True))
                a=jnp.exp(m-mn)
                p=jnp.exp(s-mn)
                ls[h]=ls[h]*a+jnp.sum(p,axis=0,keepdims=True)
                pb=p.astype(bf)
                ps[h,kb]=pb
                mk[h,kb]=mn
                ms[h]=mn
                ots[h]=ots[h]*a+dg(kvt[kb,64:,:],pb,NN)
        def fstep(kb,carry):
            @pl.when(kb<rb)
            def _(): fwd(kb,False)
            @pl.when(kb==rb)
            def _(): fwd(kb,True)
            between(pair,kb,0)
            return carry
        lax.fori_loop(0,nkb,fstep,0)
        dot_=do.astype(f32).T
        for h in range(2):
            inv=1.0/ls[h]
            ot=ots[h]*inv
            ots[h]=ot
            ls[h]=inv
        delta=[jnp.sum(ots[h]*dot_[64*h:64*h+64,:],axis=0,keepdims=True) for h in range(2)]
        o_ref[:,cols]=jnp.concatenate([ots[0],ots[1]],axis=0).T.astype(bf)
        def bwd(kb):
            for h in range(2):
                alpha=jnp.exp(mk[h,kb]-ms[h])*ls[h]
                dp=dg(v2[kb],dom[h],NT)
                p=ps[h,kb].astype(f32)*alpha
                ds=(p*(dp-delta[h])).astype(bf)
                pn=p.astype(bf)
                acck[kb]+=dg(ds,qm[h],NN)
                accv[kb]+=dg(pn,dom[h],NN)
                dqs[h]+=dg(kvt[kb,:64,:],ds,NN)
        def bstep(kb,carry):
            @pl.when(kb<=rb)
            def _(): bwd(kb)
            between(pair,kb,1)
            return carry
        lax.fori_loop(0,nkb,bstep,0)
        dq_ref[:,cols]=(turn(jnp.concatenate([dqs[0],dqs[1]],axis=0).T,tab_ref,True)*HD**-0.5).astype(bf)
        return carry
    lax.fori_loop(0,pairs,one,0)
    for kb in range(nkb):
        k=acck[kb]; v=accv[kb]
        lane=lax.broadcasted_iota(jnp.int32,k.shape,1)<64
        dkv_ref[0,kb*B:(kb+1)*B,:]=jnp.where(lane,k+pltpu.roll(k,64,1),v+pltpu.roll(v,64,1))
    if comm: end()

def attention(b,q,do,kv,tab,comm,arrays,dp,cid):
    S=kv.shape[1]; nkb=S//B; width=q.shape[1]
    blk=pl.BlockSpec((B,width),lambda *_: (b,0))
    own=pl.BlockSpec((B,width),lambda *_: (0,0))
    kvs=pl.BlockSpec((1,S,128),lambda *_: (b,0,0))
    dkvs=pl.BlockSpec((1,S,128),lambda *_: (0,0,0))
    tabs=pl.BlockSpec(tab.shape,lambda *_: (0,0,0))
    params=dict(vmem_limit_bytes=62<<20)
    if comm: params.update(collective_id=cid,has_side_effects=True)
    return pl.pallas_call(functools.partial(attn_kernel,dp//2,width//128,comm,len(arrays)),
      grid_spec=pltpu.PrefetchScalarGridSpec(num_scalar_prefetch=0,grid=(1,),in_specs=[blk,blk,kvs,tabs]+(comm.ins if comm else []),
        out_specs=[own,own,dkvs]+(comm.outs if comm else []),
        scratch_shapes=[pltpu.VMEM((nkb,B,128),bf),pltpu.VMEM((nkb,B,128),bf),pltpu.VMEM((nkb,128,B),bf),pltpu.VMEM((nkb,B,128),f32),pltpu.VMEM((nkb,B,128),f32),
                        pltpu.VMEM((2,nkb,B,B),bf),pltpu.VMEM((2,nkb,1,B),f32),pltpu.VMEM((2,1,B),f32),pltpu.VMEM((2,1,B),f32),pltpu.VMEM((2,64,B),f32),pltpu.VMEM((2,64,B),f32)]
                       +(comm.scratch if comm else [])),
      out_shape=[jax.ShapeDtypeStruct((B,width),bf),jax.ShapeDtypeStruct((B,width),bf),jax.ShapeDtypeStruct((1,S,128),f32)]+(comm.shapes if comm else []),
      compiler_params=pltpu.CompilerParams(**params),name="attn")(q,do,kv,tab,*arrays)


def kv_gather_kernel(nz, own_ref, full_ref, send, recv):
    pos = coords(nz)
    z, x, y, c = pos
    greet(pos, ["y", "c"], nz)
    nb = own_ref.shape[0]
    sent = []

    def go(b, m, src, kind):
        cp = pltpu.make_async_remote_copy(src, full_ref.at[b, m], send.at[len(sent)], recv.at[b, m],
                                          device_id=peer(pos, kind, nz), device_id_type=MESH)
        cp.start()
        sent.append(cp)

    def wait(b, m):
        pltpu.make_async_remote_copy(full_ref.at[b, m], full_ref.at[b, m], send.at[0], recv.at[b, m],
                                     device_id=peer(pos, "c", nz), device_id_type=MESH).wait_recv()

    for b in range(nb):
        go(b, y * 2 + c, own_ref.at[b], "y")
    for b in range(nb):
        go(b, y * 2 + c, own_ref.at[b], "c")
    for b in range(nb):
        full_ref[b, y * 2 + c] = own_ref[b]
    for b in range(nb):
        m = (1 - y) * 2 + c
        wait(b, m)
        go(b, m, full_ref.at[b, m], "c")
    for b in range(nb):
        wait(b, y * 2 + 1 - c)
        wait(b, (1 - y) * 2 + 1 - c)
    for cp in sent:
        cp.wait_send()


def kv_gather(own, dp, cid):
    nb, rows, w = own.shape
    return pl.pallas_call(
        functools.partial(kv_gather_kernel, dp // 2),
        in_specs=[pl.BlockSpec(memory_space=pltpu.VMEM)],
        out_specs=pl.BlockSpec(memory_space=pltpu.VMEM),
        out_shape=jax.ShapeDtypeStruct((nb, 4, rows, w), own.dtype),
        scratch_shapes=[pltpu.SemaphoreType.DMA((3 * nb,)), pltpu.SemaphoreType.DMA((nb, 4))],
        compiler_params=pltpu.CompilerParams(collective_id=cid, has_side_effects=True),
        name="gather_keyval",
    )(own)


def kv_reduce_kernel(nz, parts_ref, out_ref, low, cbuf, ybuf, ysend, send, crecv, yrecv):
    pos = coords(nz)
    z, x, y, c = pos
    greet(pos, ["y", "c"], nz)
    nb = parts_ref.shape[0]
    sent = []

    def go(src, dst, sem, kind):
        cp = pltpu.make_async_remote_copy(src, dst, send.at[len(sent)], sem, device_id=peer(pos, kind, nz), device_id_type=MESH)
        cp.start()
        sent.append(cp)

    def wait(dst, sem):
        pltpu.make_async_remote_copy(dst, dst, send.at[0], sem, device_id=peer(pos, "c", nz), device_id_type=MESH).wait_recv()

    for ry in (1, 0):
        yy = 1 - y if ry else y
        for b in range(nb):
            low[b, ry] = parts_ref[b, yy * 2 + 1 - c].astype(bf)
            go(low.at[b, ry], cbuf.at[b, ry], crecv.at[b, ry], "c")
    for b in range(nb):
        wait(cbuf.at[b, 1], crecv.at[b, 1])
        ysend[b] = (parts_ref[b, (1 - y) * 2 + c] + cbuf[b, 1].astype(f32)).astype(bf)
        go(ysend.at[b], ybuf.at[b], yrecv.at[b], "y")
    for b in range(nb):
        wait(cbuf.at[b, 0], crecv.at[b, 0])
        wait(ybuf.at[b], yrecv.at[b])
        out_ref[b] = parts_ref[b, y * 2 + c] + cbuf[b, 0].astype(f32) + ybuf[b].astype(f32)
    for cp in sent:
        cp.wait_send()


def kv_reduce(parts, dp, cid):
    nb, mp, rows, w = parts.shape
    return pl.pallas_call(
        functools.partial(kv_reduce_kernel, dp // 2),
        in_specs=[pl.BlockSpec(memory_space=pltpu.VMEM)],
        out_specs=pl.BlockSpec(memory_space=pltpu.VMEM),
        out_shape=jax.ShapeDtypeStruct((nb, rows, w), f32),
        scratch_shapes=[pltpu.VMEM((nb, 2, rows, w), bf), pltpu.VMEM((nb, 2, rows, w), bf), pltpu.VMEM((nb, rows, w), bf),
                        pltpu.VMEM((nb, rows, w), bf), pltpu.SemaphoreType.DMA((3 * nb,)), pltpu.SemaphoreType.DMA((nb, 2)), pltpu.SemaphoreType.DMA((nb,))],
        compiler_params=pltpu.CompilerParams(collective_id=cid, has_side_effects=True),
        name="reduce_keyval",
    )(parts)


def spread(arrays, inside, dp, mp):
    out = []
    for i, s in enumerate(arrays):
        if i in inside:
            out.append(lax.all_gather(s, "dp"))
        else:
            a = lax.all_gather(s, ("dp", "mp")).reshape((dp, mp) + s.shape)
            out.append(a.transpose(0, 2, 1, 3).reshape(dp, s.shape[0], -1))
    return out


def collect(parts, inside, dp, mp):
    out = []
    for i, p in enumerate(parts):
        p = p.astype(f32)
        if i in inside:
            out.append(lax.psum(lax.psum_scatter(p, "dp", scatter_dimension=0), "mp"))
        else:
            a = p.reshape(dp, p.shape[1], mp, -1).transpose(0, 2, 1, 3).reshape(dp * mp, p.shape[1], -1)
            out.append(lax.psum_scatter(a, ("dp", "mp"), scatter_dimension=0))
    return out


def rotary(position):
    lane = jnp.arange(2 * HD, dtype=jnp.int32)
    inside = lane % HD
    frequency = 10000.0 ** (-2.0 * (inside % (ROT // 2)).astype(f32) / ROT)
    angle = position[:, None].astype(f32) * frequency[None, :]
    turned = (inside < ROT)[None, :]
    low = (inside < ROT // 2)[None, :]
    cosine = jnp.where(turned, jnp.cos(angle), 1.0)
    sine = jnp.where(turned, jnp.sin(angle), 0.0)
    return jnp.stack([cosine, jnp.where(low, -sine, 0.0), jnp.where(low, 0.0, sine)])


def rotate(v, tables, back=False):
    cosine, up, down = tables
    half = ROT // 2
    a = jnp.roll(v, -half, axis=1) * up
    b = jnp.roll(v, half, axis=1) * down
    return v * cosine - a - b if back else v * cosine + a + b


def shards(tokens, norm_gains, norm_biases, w_query, w_keyval, w_output, w_up, w_down, cotangent, subset_ids, subset_weights):
    dp, mp = lax.axis_size("dp"), lax.axis_size("mp")
    me = lax.axis_index("mp")
    nb, own, width = tokens.shape
    rows = nb * own
    part = w_query.shape[0]
    cols = w_query.shape[1]
    ff = w_up.shape[1]
    mine = dp == 8
    dot = functools.partial(jnp.dot, preferred_element_type=f32)
    nt = lambda a, b: lax.dot_general(a, b, (((1,), (1,)), ((), ())), preferred_element_type=f32)
    tn = lambda a, b: lax.dot_general(a, b, (((0,), (0,)), ((), ())), preferred_element_type=f32)
    qo = jnp.concatenate([w_query, w_output], axis=1)
    kvg = jnp.concatenate([w_keyval, norm_gains, norm_biases, jnp.zeros((part, 124), bf)], axis=1)
    if mine:
        qo, kvg = communicate(Gather([qo, kvg], [(0, 0, 256, "zyx"), (0, 256, 384, "xzy"), (1, 0, 256, "zx")], dp, mp), [qo, kvg], 1, "gather_weights")
    else:
        qo, kvg = spread([qo, kvg], {1}, dp, mp)
    qo = qo.reshape(width, mp, 2 * cols)
    wq = qo[:, :, :cols].reshape(width, width)
    wo = qo[:, :, cols:].reshape(width, width)
    kvg = kvg.reshape(width, -1)
    wkv = kvg[:, : 2 * HD]
    small = kvg[:, 2 * HD : 2 * HD + 4].astype(f32).T
    gain_a, gain_m, bias_a, bias_m = small[0], small[1], small[2], small[3]

    ids = lax.dynamic_slice_in_dim(subset_ids.reshape(nb, mp * own), me * own, own, 1).reshape(rows)
    matches = ids[:, None] == jnp.arange(subset_weights.shape[0], dtype=jnp.int32)[None, :]
    scale = jnp.sum(jnp.where(matches, subset_weights[None, :], 0.0), axis=1, keepdims=True)
    grad_rows = cotangent.reshape(rows, width).astype(f32) * scale
    g = grad_rows.astype(bf)

    x = tokens.reshape(rows, width).astype(f32)
    centered = x - jnp.mean(x, axis=1, keepdims=True)
    inverse = lax.rsqrt(jnp.mean(centered * centered, axis=1, keepdims=True) + epsilon)
    normed = centered * inverse
    attn_in = (normed * gain_a + bias_a).astype(bf)
    mlp_in = (normed * gain_m + bias_m).astype(bf)
    tables = rotary(me * own + jnp.arange(own, dtype=jnp.int32))
    first = (jnp.arange(2 * HD) < HD)[None, :]
    kv_tables = [jnp.tile(jnp.where(first, t, e), (nb, 1)) for t, e in zip(tables, (1.0, 0.0, 0.0))]
    q = dot(attn_in, wq)
    kv = rotate(dot(attn_in, wkv), kv_tables).astype(bf)
    kv_full = kv_gather(kv.reshape(nb, own, 2 * HD), dp, 3).reshape(nb, mp * own, 2 * HD)
    grad_heads = dot(g, wo).astype(bf)
    mlp_plan = lambda a, b: [(0, 0, 768, a), (1, 0, 256, a), (1, 256, 768, b)]
    if mine:
        o0, dq0, dkv0, up, down = attention(0, q, grad_heads, kv_full, tables, Gather([w_up, w_down], mlp_plan("zyx", "xzy"), dp, mp), [w_up, w_down], dp, 5)
    else:
        o0, dq0, dkv0 = attention(0, q, grad_heads, kv_full, tables, None, [], dp, 5)
        up, down = spread([w_up, w_down], (), dp, mp)
    up = up.reshape(width, mp * ff)
    down = down.reshape(width, mp * ff)

    pre = dot(mlp_in, up)
    cdf = 0.5 * (1.0 + lax.erf(pre * sqrt_half))
    hidden = (pre * cdf).astype(bf)
    slope = cdf + pre * (jnp.exp(-0.5 * pre * pre) * inv_sqrt_two_pi)
    dpre = (dot(g, down) * slope).astype(bf)
    gup = tn(mlp_in, dpre).astype(bf).reshape(dp, part, mp * ff)
    gdown = tn(g, hidden).astype(bf).reshape(dp, part, mp * ff)
    if mine:
        o1, dq1, dkv1, grad_up, grad_down = attention(1, q, grad_heads, kv_full, tables, Scatter([gup, gdown], mlp_plan("xyz", "yzx"), dp, mp), [gup, gdown], dp, 6)
    else:
        o1, dq1, dkv1 = attention(1, q, grad_heads, kv_full, tables, None, [], dp, 6)
        grad_up, grad_down = collect([gup, gdown], (), dp, mp)
    dkv = kv_reduce(jnp.concatenate([dkv0, dkv1]).reshape(nb, mp, own, 2 * HD), dp, 4).reshape(rows, 2 * HD)
    o = jnp.concatenate([o0, o1])
    dqp = jnp.concatenate([dq0, dq1])

    out = (x + nt(o, wo) + nt(hidden, down)).astype(bf)
    dmlp = nt(dpre, up)
    dkvp = rotate(dkv, kv_tables, True).astype(bf)
    dattn = nt(dqp, wq) + nt(dkvp, wkv)
    dnormed = dattn * gain_a + dmlp * gain_m
    dx = (dnormed - jnp.mean(dnormed, axis=1, keepdims=True) - normed * jnp.mean(dnormed * normed, axis=1, keepdims=True)) * inverse
    input_grad = (grad_rows + dx).astype(bf)
    sums = jnp.stack([jnp.sum(dattn * normed, axis=0), jnp.sum(dmlp * normed, axis=0), jnp.sum(dattn, axis=0), jnp.sum(dmlp, axis=0)], axis=1)
    split = lambda a: a.astype(bf).reshape(width, mp, cols)
    gqo = jnp.concatenate([split(tn(attn_in, dqp)), split(tn(g, o))], axis=2).reshape(dp, part, -1)
    gkvg = jnp.concatenate([tn(attn_in, dkvp), sums, jnp.zeros((width, 124), f32)], axis=1).astype(bf).reshape(dp, part, -1)
    if mine:
        a, c = communicate(Scatter([gqo, gkvg], [(0, 0, 256, "xyz"), (0, 256, 384, "yzx"), (1, 0, 256, "xz")], dp, mp), [gqo, gkvg], 2, "scatter_grads")
    else:
        a, c = collect([gqo, gkvg], {1}, dp, mp)
    k = 2 * HD
    return (
        out.reshape(tokens.shape),
        kv_full.reshape(-1, 2 * HD),
        input_grad.reshape(tokens.shape),
        c[:, k : k + 2],
        c[:, k + 2 : k + 4],
        a[:, :cols],
        c[:, :k],
        a[:, cols:],
        grad_up,
        grad_down,
    )


def solution(mesh):
    rows = P(None, ("dp", "mp"), None)
    d, dm = P("dp", None), P("dp", "mp")
    return jax.shard_map(
        shards,
        mesh=mesh,
        in_specs=(rows, d, d, dm, d, dm, dm, dm, rows, P("dp"), P()),
        out_specs=(rows, d, rows, d, d, dm, d, dm, dm, dm),
        check_vma=False,
    )
```

time: 539 us -> 443 us (0.82)
  Pallas kernels: 314 us -> 262 us
  other arithmetic: 65.9 us -> 30.4 us
  matrix products: 89.4 us -> 76.2 us
    pallas_call x1, Pallas kernels: 102 us -> 34.9 us  [kv_reduce(): pl.pallas_call(functools.partial(kv_reduce_kernel, dp // 2), in_specs=[pl...]
    convert_element_type x2, other arithmetic: 29.6 us -> 5.74 us  [the longest x1 3.6 us: shards(): input_grad = (grad_rows + dx).astype(bf)]
    pallas_call x3 -> x4, Pallas kernels: 199 us -> 215 us  [the longest x2 153 us: attention(): pl.pallas_call(functools.partial(attn_kernel, dp // 2, width // 128, comm...]
    concatenate x5 -> x3, local copies, waits for them, and re-layouts: 17.2 us -> 1.32 us  [the longest x1 1.19 us: shards(): o = jnp.concatenate([o0, o1])]
    reshape x3 -> x4, local copies, waits for them, and re-layouts: 6.41 us -> 16.9 us  [the longest x2 6.18 us: shards(): split = lambda a: a.astype(bf).reshape(width, mp, cols)]
    dot_general x11 -> x5, matrix products: 30.7 us -> 22.3 us  [shards(): lax.dot_general(a, b, (((0,), (0,)), ((), ())), preferred_element_type=f32)]
    dot_general x11 -> x5, matrix products: 29.7 us -> 21.7 us  [shards(): lax.dot_general(a, b, (((1,), (1,)), ((), ())), preferred_element_type=f32)]
    another operation x1, other arithmetic: 8.42 us -> 0.93 us  [rotary(): jnp.stack([cosine, jnp.where(low, -sine, 0.0), jnp.where(low, 0.0, sine)])]
where the time goes in v2:
time: 443 us; the launch traced here: 438 us
  Pallas kernels  262 us (59%)
  matrix products  76.2 us (17%)
  local copies, waits for them, and re-layouts  67.8 us (15%)
  other arithmetic  30.4 us (7%)
    pallas_call x2, Pallas kernels, attention(): pl.pallas_call(functools.partial(attn_kernel, dp // 2, width // 128, comm...  153 us
    pallas_call x2, Pallas kernels, communicate(): pl.pallas_call(functools.partial(comm_kernel, comm.nz, comm, len(arrays))...  62.3 us
    pallas_call x1, Pallas kernels, kv_reduce(): pl.pallas_call(functools.partial(kv_reduce_kernel, dp // 2), in_specs=[pl...  34.9 us
    dot_general x5, matrix products, shards(): lax.dot_general(a, b, (((0,), (0,)), ((), ())), preferred_element_type=f32)  22.3 us
    dot_general x5, matrix products, shards(): lax.dot_general(a, b, (((1,), (1,)), ((), ())), preferred_element_type=f32)  21.7 us
    unnamed x106, local copies, waits for them, and re-layouts  19.3 us
    dot_general x1, matrix products, shards(): dpre = (dot(g, down) * slope).astype(bf)  12.5 us
    pallas_call x1, Pallas kernels, kv_gather(): pl.pallas_call(functools.partial(kv_gather_kernel, dp // 2), in_specs=[pl...  12 us

profile of v2, /device:TPU:0, one launch (start us, length us, event | category | flops | bytes accessed | tf_op | source)
XLA Modules:
  0.0 437.8 jit_solution(10743442900434752961)
XLA Ops:
  5.4 29.5 %gather_weights.1 = (bf16[8,96,1536]{2,1,0:T(8,128)(2,1)}, bf16[8,96,256]{2,1,0:T(8,128)(2,1)}) custom-call(bf16[96,384]{1,0:T(8,128)(2,1)} %pad_maximum_fusion.3.refs_0_, bf16[96,256]{1,0:T(8,128)(2,1)} %maximum_maximum_fusion.refs_1_), custom_call_target="tpu_custom_call" | custom-call | tf_op jit(solution)/shard_map/gather_weights/pallas_call | solution.py:264
  38.4 2.1 fusion.25
  49.4 2.0 copy.57
  51.4 2.6 fusion.39
  55.8 12.0 %gather_keyval.1 = bf16[2,4,512,128]{3,2,1,0:T(8,128)(2,1)} custom-call(bf16[2,512,128]{2,1,0:T(8,128)(2,1)} %bitcast.146), custom_call_target="tpu_custom_call" | custom-call | tf_op jit(solution)/shard_map/gather_keyval/pallas_call | solution.py:431
  67.9 2.0 fusion.11
  69.9 5.6 %reshape.717 = bf16[768,4,384]{2,1,0:T(4,128)(2,1)} reshape(bf16[8,96,1536]{2,1,0:T(8,128)(2,1)} %get-tuple-element.25) | data formatting | bytes 4718592 | tf_op jit(solution)/shard_map/reshape | solution.py:549
  75.5 5.1 %fusion.78 = (bf16[768,4,192]{2,1,0:T(4,128)(2,1)}, bf16[768,4,192]{2,1,0:T(4,128)(2,1)}) fusion(bf16[768,4,384]{2,1,0:T(4,128)(2,1)} %reshape.717), kind=kLoop, calls=%fused_computation.132 | loop fusion | bytes 4718592 | tf_op jit(solution)/shard_map/slice | solution.py:551
  80.6 3.6 copy.70
  84.2 4.3 fusion.85.refs_0_
  92.2 2.7 copy.71
  95.9 4.0 convolution_convert_fusion.2.refs_1_
  99.8 68.0 %attn.2 = (bf16[512,768]{1,0:T(8,128)(2,1)}, bf16[512,768]{1,0:T(8,128)(2,1)}, f32[1,2048,128]{2,1,0:T(8,128)}, bf16[8,96,3072]{2,1,0:T(8,128)(2,1)}, bf16[8,96,3072]{2,1,0:T(8,128)(2,1)}) custom-call(f32[1024,768]{1,0:T(8,128)} %fusion.85.refs_0_, bf16[1024,768]{1,0:T(8,128)(2,1)} %convolution_convert_fusion.2.refs_1_, bf16[2,2048,128]{2,1,0:T(8,128)(2,1)} %bitcast.119, ...), custom_call_target="tpu_custom_call" | custom-call | tf_op jit(solution)/shard_map/attn/pallas_call | solution.py:385
  167.8 10.7 %multiply_convert_fusion = (bf16[1024,3072]{1,0:T(8,128)(2,1)S(1)}, f32[1024,3072]{1,0:T(8,128)}) fusion(bf16[1024,768]{1,0:T(8,128)(2,1)} %bitcast.139, bf16[768,3072]{1,0:T(8,128)(2,1)} %bitcast.161), kind=kOutput, calls=%fused_computation.7 | convolution fusion | flops 4847566848 | bytes 25165824 | tf_op jit(solution)/shard_map/dot_general | solution.py:585
  178.5 12.5 %fusion.5 = bf16[1024,3072]{1,0:T(8,128)(2,1)S(1)} fusion(f32[1024,3072]{1,0:T(8,128)} %get-tuple-element.113, bf16[1024,768]{1,0:T(8,128)(2,1)S(1)} %bitcast.138, bf16[768,3072]{1,0:T(8,128)(2,1)S(1)} %bitcast.160), kind=kOutput, calls=%fused_computation.6 | convolution fusion | flops 4863295488 | bytes 25165824 | tf_op jit(solution)/shard_map/dot_general | solution.py:589
  191.1 6.9 %convolution_convert_fusion.1 = bf16[768,3072]{1,0:T(8,128)(2,1)} fusion(bf16[1024,768]{1,0:T(8,128)(2,1)S(1)} %copy-done.21, bf16[1024,3072]{1,0:T(8,128)(2,1)S(1)} %fusion.5), kind=kOutput, calls=%fused_computation.10 | convolution fusion | flops 4834197504 | bytes 12582912 | tf_op jit(solution)/shard_map/dot_general | solution.py:542
  198.4 7.2 %convolution_convert_fusion = bf16[768,3072]{1,0:T(8,128)(2,1)} fusion(bf16[1024,768]{1,0:T(8,128)(2,1)S(1)} %fusion.35, bf16[1024,3072]{1,0:T(8,128)(2,1)S(1)} %get-tuple-element.112), kind=kOutput, calls=%fused_computation.9 | convolution fusion | flops 4834197504 | bytes 12582912 | tf_op jit(solution)/shard_map/dot_general | solution.py:542
  205.6 84.8 %attn.3 = (bf16[512,768]{1,0:T(8,128)(2,1)}, bf16[512,768]{1,0:T(8,128)(2,1)}, f32[1,2048,128]{2,1,0:T(8,128)}, f32[96,768]{1,0:T(8,128)}, f32[96,768]{1,0:T(8,128)}) custom-call(f32[1024,768]{1,0:T(8,128)} %fusion.85.refs_0_, bf16[1024,768]{1,0:T(8,128)(2,1)} %convolution_convert_fusion.2.refs_1_, bf16[2,2048,128]{2,1,0:T(8,128)(2,1)} %bitcast.120, ...), custom_call_target="tpu_custom_call" | custom-call | tf_op jit(solution)/shard_map/attn/pallas_call | solution.py:385
  290.4 3.1 pad_maximum_fusion.1
  293.5 34.9 %reduce_keyval.1 = f32[2,512,128]{2,1,0:T(8,128)} custom-call(f32[2,4,512,128]{3,2,1,0:T(8,128)} %bitcast.122), custom_call_target="tpu_custom_call" | custom-call | tf_op jit(solution)/shard_map/reduce_keyval/pallas_call | solution.py:476
  339.4 8.2 %fusion.75 = (bf16[768]{0:T(1024)(128)(2,1)}, bf16[768]{0:T(1024)(128)(2,1)}, f32[1024]{0:T(1024)}, f32[1024]{0:T(1024)S(1)}, f32[1024,768]{1,0:T(8,128)}, /*index=5*/bf16[768]{0:T(1024)(128)(2,1)}, bf16[768]{0:T(1024)(128)(2,1)}) fusion(f32[1024]{0:T(1024)S(1)} %bitcast.153, f32[1024]{0:T(1024)S(1)} %bitcast.156, bf16[2,512,768]{2,1,0:T(8,128)(2,1)S(1)} %copy-done, ...), kind=kOutput, calls=%fused_computation.129 | convolution fusion | flops 4843628544 | bytes 18903040 | tf_op jit(solution)/shard_map/dot_general | solution.py:541
  354.5 2.3 concatenate.82.refs_1_
  356.8 3.9 convolution_convert_fusion.4
  360.7 2.6 copy.59
  365.9 2.5 convolution_convert_fusion.3
  368.4 3.6 copy.60
  372.0 4.8 %pad_maximum_fusion = bf16[768,4,384]{2,1,0:T(4,128)(2,1)} fusion(bf16[768,4,192]{2,1,0:T(4,128)(2,1)} %copy.60, bf16[768,4,192]{2,1,0:T(4,128)(2,1)S(1)} %copy.59), kind=kLoop, calls=%fused_computation.48 | loop fusion | flops 4718592 | bytes 4718592 | tf_op jit(solution)/shard_map/concatenate | solution.py:610
  376.8 5.2 %reshape.733.refs_0_ = bf16[8,96,1536]{2,1,0:T(8,128)(2,1)} reshape(bf16[768,4,384]{2,1,0:T(4,128)(2,1)} %pad_maximum_fusion) | data formatting | bytes 4718592 | tf_op jit(solution)/shard_map/reshape | solution.py:610
  382.0 32.8 %scatter_grads.1 = (f32[96,384]{1,0:T(8,128)}, f32[96,256]{1,0:T(8,128)}) custom-call(bf16[8,96,1536]{2,1,0:T(8,128)(2,1)} %reshape.733.refs_0_, bf16[8,96,256]{2,1,0:T(8,128)(2,1)} %concatenate.82.refs_1_), custom_call_target="tpu_custom_call" | custom-call | tf_op jit(solution)/shard_map/scatter_grads/pallas_call | solution.py:264
  420.2 3.6 fusion.30
  423.8 8.7 %fusion.86 = f32[1024,768]{1,0:T(8,128)S(1)} fusion(bf16[1024,3072]{1,0:T(8,128)(2,1)} %copy-done.39, bf16[768,3072]{1,0:T(8,128)(2,1)} %bitcast.159), kind=kOutput, calls=%fused_computation.140 | convolution fusion | flops 4831838208 | bytes 14155776 | tf_op jit(solution)/shard_map/dot_general | solution.py:541
  432.6 2.6 fusion.34
  (154 shorter events, 51.7 us)
Async XLA Ops:
  0.6 37.1 %copy-start = (bf16[2,512,768]{2,1,0:T(8,128)(2,1)S(1)}, bf16[2,512,768]{2,1,0:T(8,128)(2,1)}, u32[]{:S(2)}) copy-start(bf16[2,512,768]{2,1,0:T(8,128)(2,1)} %param.11) | copy-start | bytes 4718596
  37.7 4.0 copy-start.25
  45.6 8.5 %copy-start.10 = (f32[2,512,128]{2,1,0:T(8,128)}, f32[2,512,128]{2,1,0:T(8,128)S(1)}, u32[]{:S(2)}) copy-start(f32[2,512,128]{2,1,0:T(8,128)S(1)} %tile.12) | copy-start | bytes 1572868
  47.6 6.5 %copy-start.12 = (f32[2,512,128]{2,1,0:T(8,128)}, f32[2,512,128]{2,1,0:T(8,128)S(1)}, u32[]{:S(2)}) copy-start(f32[2,512,128]{2,1,0:T(8,128)S(1)} %tile.14) | copy-start | bytes 1572868
  69.9 14.3 %copy-start.8 = (bf16[2,512,768]{2,1,0:T(8,128)(2,1)}, bf16[2,512,768]{2,1,0:T(8,128)(2,1)S(1)}, u32[]{:S(2)}) copy-start(bf16[2,512,768]{2,1,0:T(8,128)(2,1)S(1)} %get-tuple-element.88) | copy-start | bytes 4718596
  84.2 6.3 %copy-start.35 = (s32[4096]{0:T(1024)S(1)}, s32[4096]{0:T(1024)}, u32[]{:S(2)}) copy-start(s32[4096]{0:T(1024)} %param.20) | copy-start | bytes 49156
  84.2 6.4 %copy-start.37 = (f32[22]{0:T(128)S(1)}, f32[22]{0:T(128)}, u32[]{:S(2)}) copy-start(f32[22]{0:T(128)} %param.21) | copy-start | bytes 268
  167.8 10.7 %copy-start.20 = (bf16[2,512,768]{2,1,0:T(8,128)(2,1)S(1)}, bf16[2,512,768]{2,1,0:T(8,128)(2,1)}, u32[]{:S(2)}) copy-start(bf16[2,512,768]{2,1,0:T(8,128)(2,1)} %multiply_convert_fusion.1) | copy-start | bytes 4718596
  167.8 10.7 %copy-start.38 = (bf16[8,96,3072]{2,1,0:T(8,128)(2,1)S(1)}, bf16[8,96,3072]{2,1,0:T(8,128)(2,1)}, u32[]{:S(2)}) copy-start(bf16[8,96,3072]{2,1,0:T(8,128)(2,1)} %get-tuple-element.27) | copy-start | bytes 14155780
  178.5 19.9 %copy-start.39 = (bf16[1024,3072]{1,0:T(8,128)(2,1)}, bf16[1024,3072]{1,0:T(8,128)(2,1)S(1)}, u32[]{:S(2)}) copy-start(bf16[1024,3072]{1,0:T(8,128)(2,1)S(1)} %get-tuple-element.112) | copy-start | bytes 18874372
  178.5 12.6 %copy-start.21 = (bf16[1024,768]{1,0:T(8,128)(2,1)S(1)}, bf16[1024,768]{1,0:T(8,128)(2,1)}, u32[]{:S(2)}) copy-start(bf16[1024,768]{1,0:T(8,128)(2,1)} %get-tuple-element.86) | copy-start | bytes 4718596
  191.1 7.0 %copy-start.40 = (bf16[1024,3072]{1,0:T(8,128)(2,1)}, bf16[1024,3072]{1,0:T(8,128)(2,1)S(1)}, u32[]{:S(2)}) copy-start(bf16[1024,3072]{1,0:T(8,128)(2,1)S(1)} %fusion.5) | copy-start | bytes 18874372
  191.1 7.0 %copy-start.4 = (bf16[2,512,768]{2,1,0:T(8,128)(2,1)S(1)}, bf16[2,512,768]{2,1,0:T(8,128)(2,1)}, u32[]{:S(2)}) copy-start(bf16[2,512,768]{2,1,0:T(8,128)(2,1)} %param.19) | copy-start | bytes 4718596
  198.4 7.2 %copy-start.18 = (bf16[1024,768]{1,0:T(8,128)(2,1)}, bf16[1024,768]{1,0:T(8,128)(2,1)S(1)}, u32[]{:S(2)}) copy-start(bf16[1024,768]{1,0:T(8,128)(2,1)S(1)} %fusion.35) | copy-start | bytes 4718596
  293.5 37.9 %copy-start.9 = (bf16[2,512,768]{2,1,0:T(8,128)(2,1)S(1)}, bf16[2,512,768]{2,1,0:T(8,128)(2,1)}, u32[]{:S(2)}) copy-start(bf16[2,512,768]{2,1,0:T(8,128)(2,1)} %copy-done.8) | copy-start | bytes 4718596
  328.4 3.0 copy-start.1
  328.4 3.0 copy-start.15
  328.5 3.0 copy-start.17
  329.9 3.2 copy-start.28
  331.5 3.0 copy-start.24
  334.5 2.8 slice-start
  334.5 4.0 slice-start.2
  335.9 2.8 slice-start.1
  335.9 3.5 slice-start.3
  339.4 15.1 %copy-start.27 = (bf16[768,128]{1,0:T(8,128)(2,1)S(1)}, bf16[768,128]{1,0:T(8,128)(2,1)}, u32[]{:S(2)}) copy-start(bf16[768,128]{1,0:T(8,128)(2,1)} %fusion.36) | copy-start | bytes 589828
  339.4 17.4 %copy-start.7 = (bf16[1024,768]{1,0:T(8,128)(2,1)S(1)}, bf16[1024,768]{1,0:T(8,128)(2,1)}, u32[]{:S(2)}) copy-start(bf16[1024,768]{1,0:T(8,128)(2,1)} %copy-done.6) | copy-start | bytes 4718596
  376.8 43.4 %copy-start.36 = (f32[1024]{0:T(1024)S(1)}, f32[1024]{0:T(1024)}, u32[]{:S(2)}) copy-start(f32[1024]{0:T(1024)} %get-tuple-element.79) | copy-start | bytes 12292
  376.8 43.4 %copy-start.5 = (bf16[2,512,768]{2,1,0:T(8,128)(2,1)S(1)}, bf16[2,512,768]{2,1,0:T(8,128)(2,1)}, u32[]{:S(2)}) copy-start(bf16[2,512,768]{2,1,0:T(8,128)(2,1)} %param.19) | copy-start | bytes 4718596
  423.8 8.7 %copy-start.23 = (bf16[768,4,192]{0,2,1:T(8,128)(2,1)S(1)}, bf16[768,4,192]{0,2,1:T(8,128)(2,1)}, u32[]{:S(2)}) copy-start(bf16[768,4,192]{0,2,1:T(8,128)(2,1)} %copy-done.22) | copy-start | bytes 3538948
  423.8 8.8 %copy-start.32 = (bf16[1024,768]{1,0:T(8,128)(2,1)S(1)}, bf16[1024,768]{1,0:T(8,128)(2,1)}, u32[]{:S(2)}) copy-start(bf16[1024,768]{1,0:T(8,128)(2,1)} %copy-done.31) | copy-start | bytes 4718596
  432.5 3.6 copy-start.34
  432.6 4.3 copy-start.33
  (13 other events, 21.9 us)
